TPU v7x, 32 devices: a whole 2x2x4 slice. The times are simulated.
32 devices in a mesh: dp: 8 (over z, y), head: 4 (over x, core).
Axes of the slice: x: 2, y: 2, z: 4, core: 2. Of those that a mesh axis runs over, the one named last changes fastest.
Arguments:
- layer_input: bfloat16 [12288, 1024], P('dp'), may hold values from -6 to 6
- proj_weight: bfloat16 [4, 1024, 1024], P(None, None, 'head'), may hold values from -0.1875 to 0.1875
- conv_weight: float32 [3, 4, 1024], P(None, None, 'head'), may hold values from -3 to 3
- persist_kv: float32 [2, 16, 16, 64], P(None, 'head'), may hold values from -4 to 4
- memory_in: float32 [16, 64, 256], P('head'), may hold values from -4 to 4
- memory_out: float32 [16, 256, 64], P('head'), may hold values from -0.375 to 0.375
- memory_gate: float32 [1024, 3, 16], P(None, None, 'head'), may hold values from -3 to 3
- out_weight: bfloat16 [1024, 1024], P(None, 'head'), may hold values from -0.375 to 0.375
- ffn_in: bfloat16 [2, 1024, 4096], P(None, None, 'head'), may hold values from -0.1875 to 0.1875
- ffn_out: bfloat16 [4096, 1024], P('head'), may hold values from -0.09375 to 0.09375
- norm_gains: float32 [2, 1024], replicated, may hold values from 0.5 to 1.5
- seq_len: int32 [8], P('dp'), may hold values from 192 to 1536, as said below
- out_grad: bfloat16 [12288, 1024], P('dp', 'head'), may hold values from -6 to 6
Outputs:
- layer_output: bfloat16 [12288, 1024], P('dp', 'head')
- input_grad: float32 [12288, 1024], P('dp', 'head')
- proj_grad: float32 [4, 1024, 1024], P(None, None, 'head')
- conv_grad: float32 [3, 4, 1024], P(None, None, 'head')
- persist_grad: float32 [2, 16, 16, 64], P(None, 'head')
- memory_in_grad: float32 [16, 64, 256], P('head')
- memory_out_grad: float32 [16, 256, 64], P('head')
- memory_gate_grad: float32 [1024, 3, 16], P(None, None, 'head')
- out_weight_grad: float32 [1024, 1024], P(None, 'head')
- ffn_in_grad: float32 [2, 1024, 4096], P(None, None, 'head')
- ffn_out_grad: float32 [4096, 1024], P('head')
- gains_grad: float32 [2, 1024], replicated
Inputs may be any that keep to these rules, and one draw needn't show every extreme that they name: Tokens of sequence g are its first seq_len[g] positions; some sequence fills all 1536 positions.
All inputs are finite; a program needn't handle non-finite values.
Results may differ from a plain program's by a relative error of at most 0.02.
Values may be sent and summed in bfloat16 or wider, within the bound.
No kernel may reach another device: no remote copies, remote signals or barrier semaphores. Data moves between devices by JAX's collectives and lax.ppermute only.
A program may use at most 384 MiB of HBM per device.

v0:
```python
import jax
import jax.numpy as jnp
from jax import lax
from jax.sharding import PartitionSpec as P

HS = 64
SPAN = 512


HIGH = lax.Precision.HIGHEST
NORM_EPS = 1e-05
UNIT_EPS = 1e-06
SCORE_SCALE = 8.0
MASKED = -1e30


def memory_net(rows_in, first_layer, second_layer):
    return jnp.dot(
        jax.nn.silu(jnp.dot(rows_in, first_layer, precision=HIGH)), second_layer, precision=HIGH
    )


def memory_head(queries, keys_in, values_in, logits, first_layer, second_layer, valid_rows):
    span_count = logits.shape[0]
    span_rows = queries.shape[0] // span_count

    def advance(state_now, span_item):
        first_now, second_now, moment_one, moment_two = state_now
        query_span, key_span, value_span, logit_span, valid_span = span_item
        recalled = memory_net(query_span, first_now, second_now)
        counted = jnp.maximum(jnp.sum(valid_span), 1.0)

        def inner_loss(first_try, second_try):
            residue = memory_net(key_span, first_try, second_try) - value_span
            return jnp.sum(valid_span[:, None] * residue * residue) / (2.0 * counted)

        grad_one, grad_two = jax.grad(inner_loss, argnums=(0, 1))(first_now, second_now)
        step_size = 0.2 * jax.nn.sigmoid(logit_span[0])
        momentum_keep = jax.nn.sigmoid(logit_span[1])
        forget = 0.5 * jax.nn.sigmoid(logit_span[2])
        moment_one = momentum_keep * moment_one - step_size * grad_one
        moment_two = momentum_keep * moment_two - step_size * grad_two
        first_next = (1.0 - forget) * first_now + moment_one
        second_next = (1.0 - forget) * second_now + moment_two
        return ((first_next, second_next, moment_one, moment_two), recalled)

    initial = (first_layer, second_layer, jnp.zeros_like(first_layer), jnp.zeros_like(second_layer))
    span_items = (
        queries.reshape(span_count, span_rows, -1),
        keys_in.reshape(span_count, span_rows, -1),
        values_in.reshape(span_count, span_rows, -1),
        logits,
        valid_rows.reshape(span_count, span_rows),
    )
    final_state, recalled = lax.scan(advance, initial, span_items)
    return recalled.reshape(queries.shape[0], -1)


def memory_all(
    queries, keys_in, values_in, normed, gate_weight, first_layer, second_layer, valid_rows
):
    span_count = queries.shape[0] // SPAN
    width = normed.shape[1]
    grouped = normed.reshape(span_count, SPAN, width)
    valid_grouped = valid_rows.reshape(span_count, SPAN)
    counted = jnp.maximum(jnp.sum(valid_grouped, 1), 1.0)
    means = jnp.einsum("ctd,ct->cd", grouped, valid_grouped, precision=HIGH) / counted[:, None]
    logits = jnp.einsum("cd,dgh->hcg", means, gate_weight, precision=HIGH)
    return jax.vmap(memory_head, in_axes=(1, 1, 1, 0, 0, 0, None), out_axes=1)(
        queries, keys_in, values_in, logits, first_layer, second_layer, valid_rows
    )


def conv_rows(values_in, kernel):
    summed = jnp.zeros_like(values_in)
    for offset in range(kernel.shape[0]):
        shifted = jnp.pad(values_in, ((offset, 0), (0, 0)))[: values_in.shape[0]]
        summed = summed + kernel[offset] * shifted
    return summed


def unit_rows(values_in):
    return values_in * lax.rsqrt(jnp.sum(values_in * values_in, -1, keepdims=True) + UNIT_EPS)


def prepare(query_pre, key_pre, value_pre, kernels):
    length = query_pre.shape[0]
    queries = unit_rows(jax.nn.silu(conv_rows(query_pre, kernels[0])).reshape(length, -1, HS))
    keys_out = unit_rows(jax.nn.silu(conv_rows(key_pre, kernels[1])).reshape(length, -1, HS))
    values_out = jax.nn.silu(conv_rows(value_pre, kernels[2])).reshape(length, -1, HS)
    return (queries, keys_out, values_out)


def persist(persist_pair):
    return (unit_rows(persist_pair[0]), persist_pair[1])


def rows_back(d_rows, rows_in, scale, gain):
    width = rows_in.shape[1]
    inner_sum = jnp.sum(d_rows * gain * rows_in, -1, keepdims=True)
    d_input = scale * gain * d_rows - rows_in * scale * scale * scale * inner_sum / width
    return (d_input, jnp.sum(d_rows * rows_in * scale, 0))


def per_device(
    layer_input,
    proj_weight,
    conv_weight,
    persist_kv,
    memory_in,
    memory_out,
    memory_gate,
    out_weight,
    ffn_in,
    ffn_out,
    norm_gains,
    seq_len,
    out_grad,
):
    rows = layer_input.shape[0]
    local_cols = proj_weight.shape[2]
    local_heads = persist_kv.shape[1]
    persist_rows = persist_kv.shape[2]
    head_size = persist_kv.shape[3]
    col_start = lax.axis_index("head") * local_cols
    rows_f32 = layer_input.astype(jnp.float32)
    scale_one = lax.rsqrt(jnp.mean(rows_f32 * rows_f32, -1, keepdims=True) + NORM_EPS)
    normed = rows_f32 * scale_one * norm_gains[0]
    normed_low = normed.astype(jnp.bfloat16)
    projected = jnp.einsum(
        "td,idf->itf", normed_low, proj_weight, preferred_element_type=jnp.float32
    )
    valid_rows = (jnp.arange(rows, dtype=jnp.int32) < seq_len[0]).astype(jnp.float32)
    prepared, prep_pull = jax.vjp(prepare, projected[0], projected[1], projected[2], conv_weight)
    query_low = prepared[0].astype(jnp.bfloat16)
    key_low = prepared[1].astype(jnp.bfloat16)
    value_low = prepared[2].astype(jnp.bfloat16)
    persisted, persist_pull = jax.vjp(persist, persist_kv)
    keys_all = jnp.concatenate(
        [persisted[0].astype(jnp.bfloat16), jnp.transpose(key_low, (1, 0, 2))], 1
    )
    values_all = jnp.concatenate(
        [persisted[1].astype(jnp.bfloat16), jnp.transpose(value_low, (1, 0, 2))], 1
    )
    block_rows = min(512, rows)
    blocks = rows // block_rows
    starts = jnp.arange(blocks, dtype=jnp.int32) * block_rows
    key_place = jnp.concatenate(
        [jnp.full((persist_rows,), -1, jnp.int32), jnp.arange(rows, dtype=jnp.int32)]
    )
    query_blocks = query_low.reshape(blocks, block_rows, local_heads, head_size)

    def block_scores(query_block, block_start):
        scores = SCORE_SCALE * jnp.einsum(
            "qhd,hkd->hqk", query_block, keys_all, preferred_element_type=jnp.float32
        )
        query_place = block_start + jnp.arange(block_rows, dtype=jnp.int32)
        allowed = key_place[None, None, :] <= query_place[None, :, None]
        return jnp.where(allowed, scores, MASKED)

    def forward_block(block_item):
        query_block, block_start = block_item
        scores = block_scores(query_block, block_start)
        top_score = jnp.max(scores, -1, keepdims=True)
        raised = jnp.exp(scores - top_score)
        totals = jnp.sum(raised, -1, keepdims=True)
        weights = (raised / totals).astype(jnp.bfloat16)
        block_out = jnp.einsum(
            "hqk,hkd->qhd", weights, values_all, preferred_element_type=jnp.float32
        )
        return (block_out, (top_score + jnp.log(totals))[..., 0])

    attended_blocks, log_totals = lax.map(forward_block, (query_blocks, starts))
    attended = attended_blocks.reshape(rows, local_heads, head_size)

    def memory_piece(query_in, key_in, value_in, normed_in, gate_in, first_in, second_in):
        return memory_all(
            query_in, key_in, value_in, normed_in, gate_in, first_in, second_in, valid_rows
        )

    recalled, memory_pull = jax.vjp(
        memory_piece,
        query_low.astype(jnp.float32),
        key_low.astype(jnp.float32),
        value_low.astype(jnp.float32),
        normed,
        memory_gate,
        memory_in,
        memory_out,
    )
    gate_act = jax.nn.sigmoid(projected[3]).reshape(rows, local_heads, head_size)
    mixed_rows = ((attended + recalled) * gate_act).reshape(rows, local_cols).astype(jnp.bfloat16)
    mixed_full = lax.all_gather(mixed_rows, "head", axis=1, tiled=True)
    branch = jnp.dot(mixed_full, out_weight, preferred_element_type=jnp.float32)
    input_cols = lax.dynamic_slice_in_dim(rows_f32, col_start, local_cols, 1)
    residual = input_cols + branch
    residual_full = lax.all_gather(residual, "head", axis=1, tiled=True)
    scale_two = lax.rsqrt(jnp.mean(residual_full * residual_full, -1, keepdims=True) + NORM_EPS)
    normed_two = (residual_full * scale_two * norm_gains[1]).astype(jnp.bfloat16)
    ffn_pre = jnp.einsum("td,idf->itf", normed_two, ffn_in, preferred_element_type=jnp.float32)
    sig_gate = jax.nn.sigmoid(ffn_pre[0])
    silu_gate = ffn_pre[0] * sig_gate
    hidden = (silu_gate * ffn_pre[1]).astype(jnp.bfloat16)
    ffn_part = jnp.dot(hidden, ffn_out, preferred_element_type=jnp.float32)
    ffn_cols = lax.psum_scatter(ffn_part, "head", scatter_dimension=1, tiled=True)
    layer_output = (residual + ffn_cols).astype(jnp.bfloat16)
    cot_cols = out_grad.astype(jnp.float32)
    cot_full = lax.all_gather(out_grad, "head", axis=1, tiled=True)
    d_hidden = lax.dot_general(
        cot_full, ffn_out, (((1,), (1,)), ((), ())), preferred_element_type=jnp.float32
    )
    ffn_out_grad = lax.dot_general(
        hidden, cot_full, (((0,), (0,)), ((), ())), preferred_element_type=jnp.float32
    )
    silu_slope = sig_gate * (1.0 + ffn_pre[0] * (1.0 - sig_gate))
    d_ffn_pre = jnp.stack([d_hidden * ffn_pre[1] * silu_slope, d_hidden * silu_gate]).astype(
        jnp.bfloat16
    )
    ffn_in_grad = jnp.einsum(
        "td,itf->idf", normed_two, d_ffn_pre, preferred_element_type=jnp.float32
    )
    d_normed_two = jnp.einsum("itf,idf->td", d_ffn_pre, ffn_in, preferred_element_type=jnp.float32)
    d_two_full = lax.psum(d_normed_two, "head")
    d_two_rows, gain_two_grad = rows_back(d_two_full, residual_full, scale_two, norm_gains[1])
    d_two_cols = lax.dynamic_slice_in_dim(d_two_rows, col_start, local_cols, 1)
    d_residual = cot_cols + d_two_cols
    d_branch = d_residual.astype(jnp.bfloat16)
    out_weight_grad = lax.dot_general(
        mixed_full, d_branch, (((0,), (0,)), ((), ())), preferred_element_type=jnp.float32
    )
    d_mixed_part = lax.dot_general(
        d_branch, out_weight, (((1,), (1,)), ((), ())), preferred_element_type=jnp.float32
    )
    d_mixed_flat = lax.psum_scatter(d_mixed_part, "head", scatter_dimension=1, tiled=True)
    d_mixed = d_mixed_flat.reshape(rows, local_heads, head_size)
    d_attended = (d_mixed * gate_act).astype(jnp.bfloat16)
    d_recalled = d_mixed * gate_act
    d_gate_pre = (d_mixed * (attended + recalled) * gate_act * (1.0 - gate_act)).reshape(
        rows, local_cols
    )

    def backward_block(grads_now, block_item):
        d_keys_now, d_values_now = grads_now
        query_block, d_out_block, log_block, block_start = block_item
        scores = block_scores(query_block, block_start)
        probs = jnp.exp(scores - log_block[..., None])
        probs_low = probs.astype(jnp.bfloat16)
        d_probs = jnp.einsum(
            "qhd,hkd->hqk", d_out_block, values_all, preferred_element_type=jnp.float32
        )
        d_values_now = d_values_now + jnp.einsum(
            "hqk,qhd->hkd", probs_low, d_out_block, preferred_element_type=jnp.float32
        )
        d_scores = (probs * (d_probs - jnp.sum(probs * d_probs, -1, keepdims=True))).astype(
            jnp.bfloat16
        )
        d_query_block = SCORE_SCALE * jnp.einsum(
            "hqk,hkd->qhd", d_scores, keys_all, preferred_element_type=jnp.float32
        )
        d_keys_now = d_keys_now + SCORE_SCALE * jnp.einsum(
            "hqk,qhd->hkd", d_scores, query_block, preferred_element_type=jnp.float32
        )
        return ((d_keys_now, d_values_now), d_query_block)

    zero_keys = jnp.zeros((local_heads, persist_rows + rows, head_size), jnp.float32)
    d_out_blocks = d_attended.reshape(blocks, block_rows, local_heads, head_size)
    (d_keys_all, d_values_all), d_query_blocks = lax.scan(
        backward_block, (zero_keys, zero_keys), (query_blocks, d_out_blocks, log_totals, starts)
    )
    (
        d_query_mem,
        d_key_mem,
        d_value_mem,
        d_normed_mem,
        memory_gate_grad,
        memory_in_grad,
        memory_out_grad,
    ) = memory_pull(d_recalled)
    d_queries = d_query_blocks.reshape(rows, local_heads, head_size) + d_query_mem
    d_keys = jnp.transpose(d_keys_all[:, persist_rows:], (1, 0, 2)) + d_key_mem
    d_values = jnp.transpose(d_values_all[:, persist_rows:], (1, 0, 2)) + d_value_mem
    d_query_pre, d_key_pre, d_value_pre, conv_grad = prep_pull((d_queries, d_keys, d_values))
    persist_grad = persist_pull((d_keys_all[:, :persist_rows], d_values_all[:, :persist_rows]))[0]
    d_projected = jnp.stack([d_query_pre, d_key_pre, d_value_pre, d_gate_pre]).astype(jnp.bfloat16)
    proj_grad = jnp.einsum(
        "td,itf->idf", normed_low, d_projected, preferred_element_type=jnp.float32
    )
    d_normed = (
        jnp.einsum("itf,idf->td", d_projected, proj_weight, preferred_element_type=jnp.float32)
        + d_normed_mem
    )
    d_one_full = lax.psum(d_normed.astype(jnp.bfloat16), "head").astype(jnp.float32)
    d_one_rows, gain_one_grad = rows_back(d_one_full, rows_f32, scale_one, norm_gains[0])
    d_one_cols = lax.dynamic_slice_in_dim(d_one_rows, col_start, local_cols, 1)
    input_grad = d_residual + d_one_cols
    gains_grad = jnp.stack([gain_one_grad, gain_two_grad])
    (
        proj_grad,
        conv_grad,
        persist_grad,
        memory_in_grad,
        memory_out_grad,
        memory_gate_grad,
        out_weight_grad,
        ffn_in_grad,
        ffn_out_grad,
        gains_grad,
    ) = lax.psum(
        (
            proj_grad,
            conv_grad,
            persist_grad,
            memory_in_grad,
            memory_out_grad,
            memory_gate_grad,
            out_weight_grad,
            ffn_in_grad,
            ffn_out_grad,
            gains_grad,
        ),
        "dp",
    )
    return (
        layer_output,
        input_grad,
        proj_grad,
        conv_grad,
        persist_grad,
        memory_in_grad,
        memory_out_grad,
        memory_gate_grad,
        out_weight_grad,
        ffn_in_grad,
        ffn_out_grad,
        gains_grad,
    )


def solution(mesh):
    in_specs = (
        P("dp", None),
        P(None, None, "head"),
        P(None, None, "head"),
        P(None, "head", None, None),
        P("head", None, None),
        P("head", None, None),
        P(None, None, "head"),
        P(None, "head"),
        P(None, None, "head"),
        P("head", None),
        P(),
        P("dp"),
        P("dp", "head"),
    )
    out_specs = (
        P("dp", "head"),
        P("dp", "head"),
        P(None, None, "head"),
        P(None, None, "head"),
        P(None, "head", None, None),
        P("head", None, None),
        P("head", None, None),
        P(None, None, "head"),
        P(None, "head"),
        P(None, None, "head"),
        P("head", None),
        P(),
    )
    return jax.shard_map(
        per_device, mesh=mesh, in_specs=in_specs, out_specs=out_specs, check_vma=False
    )
```

profile of v0, /device:TPU:0, one launch (start us, length us, event | category | flops | bytes accessed | tf_op | source)
XLA Modules:
  0.0 1930.4 jit_solution(11211905825747704570)
XLA Ops:
  79.5 151.9 %while.142 = (s32[]{:T(128)}, f32[4,64,256]{2,1,0:T(8,128)S(1)}, f32[4,256,64]{1,2,0:T(8,128)S(1)}, f32[4,64,256]{2,1,0:T(8,128)}, f32[4,256,64]{1,2,0:T(8,128)}...) while((s32[]{:T(128)}, f32[4,64,256]{2,1,0:T(8,128)S(1)}, ...), condition=%wide.region_11.12_spmd.clone, body=%wide.region_9.11_spmd.clone.sunk | while | flops 2839675392 | bytes 89542472 | solution.py:55
  93.1 9.6 bitcast_dynamic-update-slice_fusion.30
  143.6 9.6 bitcast_dynamic-update-slice_fusion.30
  242.4 105.7 %while.141 = (s32[]{:T(128)}, f32[3,512,4,64]{1,0,3,2:T(4,128)}, f32[3,4,512]{2,1,0:T(4,128)S(1)}, s32[3]{0:T(128)S(1)}, bf16[3,512,4,64]{1,3,2,0:T(8,128)(2,1)}...) while((s32[]{:T(128)}, f32[3,512,4,64]{1,0,3,2:T(4,128)}, ...), condition=%wide.region_7.8_spmd, body=%wide.region_4.7_spmd.sunk | while | flops 852630016 | bytes 49048280 | solution.py:173
  266.5 11.1 dynamic_update_slice.309
  301.7 11.1 dynamic_update_slice.309
  336.9 11.1 dynamic_update_slice.309
  364.3 25.7 %all-gather.4.cloned.1.call-done = bf16[1536,1024]{0,1:T(8,128)(2,1)} async-done(((bf16[1536,256]{0,1:T(8,128)(2,1)}), bf16[1536,1024]{0,1:T(8,128)(2,1)}) %all-gather.4.cloned.1.call-update) | async-done | bytes 3145744 | tf_op jit(solution)/shard_map/all_gather | solution.py:193
  395.4 45.8 %all-gather.6.cloned.1.call-done = f32[1536,1024]{1,0:T(8,128)} async-done(((f32[1536,256]{1,0:T(8,128)}), f32[1536,1024]{1,0:T(8,128)}) %all-gather.6.cloned.1.call-update) | async-done | bytes 6291472 | tf_op jit(solution)/shard_map/all_gather | solution.py:197
  459.1 12.5 all-gather.8.cloned.1.call-done
  471.7 11.5 fusion.167
  494.6 119.6 %all-reduce.45.cloned.1.call-done = f32[1536,1024]{1,0:T(8,128)} async-done(((f32[1536,1024]{1,0:T(8,128)}), f32[1536,1024]{1,0:T(8,128)}) %all-reduce.45.cloned.1.call-update) | async-done | bytes 6291472 | tf_op jit(solution)/shard_map/psum | solution.py:223
  631.8 54.8 %reduce-scatter.5.cloned.1.call-done = f32[1536,256]{1,0:T(8,128)} async-done(((f32[1536,1024]{1,0:T(8,128)}), f32[1536,256]{1,0:T(8,128)}) %reduce-scatter.5.cloned.1.call-update) | async-done | bytes 1572880 | tf_op jit(solution)/shard_map/reduce_scatter | solution.py:234
  699.0 148.4 %while.143 = (s32[]{:T(128)}, f32[4,1552,64]{1,2,0:T(8,128)}, f32[4,1552,64]{1,2,0:T(8,128)}, f32[3,512,4,64]{1,0,3,2:T(4,128)}, s32[3]{0:T(128)S(1)}, /*index=5...) while((s32[]{:T(128)}, f32[4,1552,64]{1,2,0:T(8,128)}, ...), condition=%wide.region_19.20_spmd.clone, body=%wide.region_17.19_spmd.clone.sunk | while | flops 2065754624 | bytes 135123184 | solution.py:267
  722.9 11.1 dynamic_update_slice.325
  771.5 11.1 dynamic_update_slice.325
  821.3 11.1 dynamic_update_slice.325
  860.4 199.4 %while.144 = (s32[]{:T(128)}, f32[4,64,256]{2,1,0:T(8,128)}, f32[4,256,64]{1,2,0:T(8,128)}, f32[4,64,256]{2,1,0:T(8,128)S(1)}, f32[4,256,64]{1,2,0:T(8,128)}, /*...) while((s32[]{:T(128)}, f32[4,64,256]{2,1,0:T(8,128)}, ...), condition=%wide.region_27.28_spmd.clone, body=%wide.region_20.27_spmd.clone.sunk | while | flops 5653331968 | bytes 116017896 | solution.py:55
  1087.8 11.8 multiply_reduce_fusion.19
  1141.0 11.2 fusion.161
  1159.4 34.4 %all-reduce.47.cloned.1.call-done = bf16[1536,1024]{1,0:T(8,128)(2,1)} async-done(((bf16[1536,1024]{1,0:T(8,128)(2,1)}), bf16[1536,1024]{1,0:T(8,128)(2,1)}) %all-reduce.47.cloned.1.call-update) | async-done | bytes 3145744 | tf_op jit(solution)/shard_map/psum | solution.py:292
  1210.2 44.8 %reduce-scatter.3.cloned.1.call-done = f32[1536,256]{1,0:T(8,128)} async-done(((f32[1536,1024]{1,0:T(8,128)}), f32[1536,256]{1,0:T(8,128)}) %reduce-scatter.3.cloned.1.call-update) | async-done | bytes 1572880 | tf_op jit(solution)/shard_map/reduce_scatter | solution.py:205
  1262.5 69.1 %all-reduce.49.cloned.1.call-done = (f32[3,4,256]{2,1,0:T(4,128)}, f32[2,4,16,64]{2,3,1,0:T(8,128)}, f32[1024,3,4]{0,2,1:T(4,128)}, f32[2,1024]{1,0:T(2,128)}) async-done(((f32[3,4,256]{2,1,0:T(4,128)}, f32[2,4,16,64]{2,3,1,0:T(8,128)}, f32[1024,3,4]{0,2,1:T(4,128)}, f32[2,1024]{1,0:T(2,128)}), (f32[3,4,256]{2,1,0:T(4,128)}, f32[2,4,16,64]{2,3,1,0:T(8,128)}, f32[1024,3,4]{0,2,1:T(4,128)}, ...) | async-done | bytes 102416 | tf_op jit(solution)/shard_map/psum | solution.py:308
  1333.2 566.2 %all-reduce.51.cloned.1.call-done = (f32[4,1024,256]{1,2,0:T(8,128)}, f32[4,64,256]{2,1,0:T(8,128)}, f32[4,256,64]{1,2,0:T(8,128)}, f32[1024,256]{1,0:T(8,128)},...) async-done(((f32[4,1024,256]{1,2,0:T(8,128)}, f32[4,64,256]{2,1,0:T(8,128)}, f32[4,256,64]{1,2,0:T(8,128)}, f32[1024,256]{1,0:T(8,128)}, f32[2,1024,1024]{1,2,0:T(8,128)}, ...) | async-done | bytes 18350096 | tf_op jit(solution)/shard_map/psum | solution.py:308
  (732 shorter events, 799.9 us)
Async XLA Ops:
  7.2 464.5 %copy-start = (bf16[1024,1024]{1,0:T(8,128)(2,1)S(1)}, bf16[1024,1024]{1,0:T(8,128)(2,1)}, u32[]{:S(2)}) copy-start(bf16[1024,1024]{1,0:T(8,128)(2,1)} %param.30) | copy-start | bytes 6291460
  7.2 382.8 %all-gather.4.cloned.1.call-start = ((), (), s32[]{:S(2)}) async-start(), calls=%async_computation.2 | async-start | bytes 3932160 | tf_op jit(solution)/shard_map/all_gather | solution.py:193
  22.8 11.7 copy-start.88
  22.8 11.7 copy-start.90
  22.8 11.7 copy-start.92
  22.8 11.7 copy-start.94
  30.1 25.6 %copy-start.65 = (f32[1536,4]{0,1:T(4,128)}, f32[1536,4]{0,1:T(4,128)S(1)}, u32[]{:S(2)}) copy-start(f32[1536,4]{0,1:T(4,128)S(1)} %multiply_reduce_fusion.22) | copy-start | bytes 73732
  55.7 181.0 %copy-start.60 = (f32[1536,4]{0,1:T(4,128)}, f32[1536,4]{0,1:T(4,128)S(1)}, u32[]{:S(2)}) copy-start(f32[1536,4]{0,1:T(4,128)S(1)} %add_rsqrt_fusion.1) | copy-start | bytes 73732
  358.6 82.5 %all-gather.6.cloned.1.call-start = ((), (), s32[]{:S(2)}) async-start(), calls=%async_computation.3 | async-start | bytes 7864320 | tf_op jit(solution)/shard_map/all_gather | solution.py:197
  358.9 31.2 %copy-start.59 = (bf16[1024,256]{1,0:T(8,128)(2,1)S(1)}, bf16[1024,256]{1,0:T(8,128)(2,1)}, u32[]{:S(2)}) copy-start(bf16[1024,256]{1,0:T(8,128)(2,1)} %param.28) | copy-start | bytes 1572868
  394.6 77.1 %all-gather.8.cloned.1.call-start = ((), (), s32[]{:S(2)}) async-start(), calls=%async_computation.5 | async-start | bytes 3932160 | tf_op jit(solution)/shard_map/all_gather | solution.py:208
  395.3 218.9 %all-reduce.45.cloned.1.call-start = ((), (), s32[]{:S(2)}) async-start(), calls=%async_computation.6 | async-start | bytes 12582912 | tf_op jit(solution)/shard_map/psum | solution.py:223
  471.7 14.1 copy-start.114
  494.5 192.0 %reduce-scatter.5.cloned.1.call-start = ((), (), s32[]{:S(2)}) async-start(), calls=%async_computation.7 | async-start | bytes 7864320 | tf_op jit(solution)/shard_map/reduce_scatter | solution.py:234
  627.8 566.0 %all-reduce.47.cloned.1.call-start = ((), (), s32[]{:S(2)}) async-start(), calls=%async_computation.8 | async-start | bytes 6291456 | tf_op jit(solution)/shard_map/psum | solution.py:292
  1087.8 11.8 copy-start.101
  1087.8 11.8 copy-start.103
  1087.8 11.8 copy-start.105
  1125.2 129.8 %reduce-scatter.3.cloned.1.call-start = ((), (), s32[]{:S(2)}) async-start(), calls=%async_computation.4 | async-start | bytes 7864320 | tf_op jit(solution)/shard_map/reduce_scatter | solution.py:205
  1132.5 199.1 %all-reduce.49.cloned.1.call-start = ((), (), s32[]{:S(2)}) async-start(), calls=%async_computation.9 | async-start | bytes 663552 | tf_op jit(solution)/shard_map/psum | solution.py:308
  1152.3 41.5 %copy-start.71 = (f32[1536]{0:T(1024)S(1)}, f32[1536]{0:T(1024)}, u32[]{:S(2)}) copy-start(f32[1536]{0:T(1024)} %copy-done.70) | copy-start | bytes 18436
  1152.3 41.5 %copy-start.76 = (f32[1,1024]{1,0:T(1,128)S(1)}, f32[1,1024]{1,0:T(1,128)}, u32[]{:S(2)}) copy-start(f32[1,1024]{1,0:T(1,128)} %copy-done.75) | copy-start | bytes 12292
  1159.4 40.6 %copy-start.83 = (f32[1024]{0:T(1024)S(1)}, f32[1024]{0:T(1024)}, u32[]{:S(2)}) copy-start(f32[1024]{0:T(1024)} %get-tuple-element.2144) | copy-start | bytes 12292
  1200.6 698.9 %all-reduce.51.cloned.1.call-start = ((), (), s32[]{:S(2)}) async-start(), calls=%async_computation.10 | async-start | bytes 36700160 | tf_op jit(solution)/shard_map/psum | solution.py:308
  (145 other events, 641.9 us)
Sparse Core Ops, SparseCore 0:
  358.7 31.2 all-gather.3
  394.7 46.3 all-gather.5
  442.7 28.9 all-gather.7
  494.6 119.5 all-reduce.44
  627.9 58.5 reduce-scatter.4
  1125.3 68.4 all-reduce.46
  1196.5 58.4 reduce-scatter.2
  1259.8 71.7 all-reduce.48
  1339.0 560.4 all-reduce.50
where the time goes:
time: 1940 us; the launch traced here: 1930 us
  waiting for transfers between devices  974 us (50%)
  matrix products  477 us (25%)
  local copies, waits for them, and re-layouts  263 us (14%)
  other arithmetic  178 us (9%)
  loops' own time  21.2 us (1%)
    psum x2, waiting for transfers between devices, per_device(): lax.psum((proj_grad, conv_grad, persist_grad, memory_in_grad, memory_out_...  635 us
    dot_general x36, matrix products, memory_net(): jnp.dot(jax.nn.silu(jnp.dot(rows_in, first_layer, precision=HIGH)), secon...  140 us
    psum x1, waiting for transfers between devices, per_device(): d_two_full = lax.psum(d_normed_two, 'head')  120 us
    dot_general x27, matrix products, memory_net(): jnp.dot(rows_in, first_layer, precision=HIGH)  119 us
    dynamic_update_slice x12, local copies, waits for them, and re-layouts, per_device(): attended_blocks, log_totals = lax.map(forward_block, (query_blocks, starts))  69.8 us
    unnamed x242, local copies, waits for them, and re-layouts  56 us
    reduce_scatter x1, waiting for transfers between devices, per_device(): lax.psum_scatter(d_mixed_part, 'head', scatter_dimension=1, tiled=True)  54.8 us
    dot_general x6, matrix products, block_scores(): jnp.einsum('qhd,hkd->hqk', query_block, keys_all, preferred_element_type=...  49.8 us
  transfers between devices with their start and end apart: 9, of which 9 were waited for; matrix products, arithmetic and copies ran while one was open for 4% of the time, Pallas kernels for 0%

commit v1 on v0

v1 whole, which is shorter than its diff:
```python
import functools

import jax
import jax.numpy as jnp
from jax import lax
from jax.experimental import pallas as pl
from jax.experimental.pallas import tpu as pltpu
from jax.sharding import PartitionSpec as P

F32 = jnp.float32
BF16 = jnp.bfloat16
HIGH = lax.Precision.HIGHEST
NORM_EPS = 1e-05
UNIT_EPS = 1e-06
SCORE_SCALE = 8.0
SPAN = 512
HALO = 8
GATE_ROWS = 128


def dot_nn(left, right):
    return jnp.dot(left, right, preferred_element_type=F32)


def dot_nt(left, right, precision=None):
    return lax.dot_general(
        left, right, (((1,), (1,)), ((), ())), preferred_element_type=F32, precision=precision
    )


def two_parts(value):
    high = value.astype(BF16)
    return high, (value - high.astype(F32)).astype(BF16)


def iota(shape, axis):
    return lax.broadcasted_iota(jnp.int32, shape, axis)


def head_blocks(cols, shift):
    same = (iota((cols, cols), 0) >> shift) == (iota((cols, cols), 1) >> shift)
    return jnp.where(same, 1.0, 0.0).astype(BF16)


def head_sum(value, blocks):
    high, rest = two_parts(value)
    return dot_nn(high, blocks) + dot_nn(rest, blocks)


def valid_column(seq_ref, start, rows):
    inside = (start + iota((rows, 1), 0)) < seq_ref[0]
    valid = jnp.where(inside, 1.0, 0.0)
    return valid, jnp.maximum(jnp.sum(valid, 0, keepdims=True), 1.0)


def head_mask(cols, shift, head):
    return jnp.where((iota((1, cols), 1) >> shift) == head, 1.0, 0.0)


def gate_rows(logits, group, heads, head_size, width):
    parts = [
        jnp.broadcast_to(
            logits[0:1, group * heads + head : group * heads + head + 1], (head_size, width)
        )
        for head in range(heads)
    ]
    return jnp.concatenate(parts, 0)


def prep_kernel(
    shift,
    seq_ref,
    x_ref,
    w_ref,
    conv_ref,
    gain_ref,
    gate_ref,
    pers_ref,
    q_ref,
    k_ref,
    v_ref,
    kt_ref,
    pre_ref,
    gp_ref,
    nl_ref,
    mean_ref,
    lg_ref,
    pers_out_ref,
    ext_ref,
):
    step = pl.program_id(0)
    rows, cols = q_ref.shape
    blocks = head_blocks(cols, shift)

    @pl.when(step == 0)
    def _():
        ext_ref[:, 0:HALO, :] = jnp.zeros((3, HALO, cols), F32)
        keys = pers_ref[0]
        keys = keys * lax.rsqrt(head_sum(keys * keys, blocks) + UNIT_EPS)
        pers_out_ref[0] = keys.astype(BF16)
        pers_out_ref[1] = pers_ref[1].astype(BF16)

    x = x_ref[...].astype(F32)
    scale = lax.rsqrt(jnp.mean(x * x, -1, keepdims=True) + NORM_EPS)
    normed = x * scale * gain_ref[0:1, :]
    low = normed.astype(BF16)
    nl_ref[...] = low
    valid, count = valid_column(seq_ref, step * rows, rows)
    mean = jnp.broadcast_to(
        jnp.sum(normed * valid, 0, keepdims=True) / count, (8, normed.shape[1])
    )
    mean_ref[...] = mean
    lg_ref[...] = dot_nt(mean, gate_ref[...], HIGH)
    gp_ref[...] = dot_nn(low, w_ref[3])
    for i in range(3):
        pre = dot_nn(low, w_ref[i])
        pre_ref[i] = pre
        ext_ref[i, HALO : HALO + rows, :] = pre
        conv = conv_ref[i, 0:1, :] * pre
        for j in range(1, conv_ref.shape[1]):
            conv = conv + conv_ref[i, j : j + 1, :] * ext_ref[i, HALO - j : HALO - j + rows, :]
        ext_ref[i, 0:HALO, :] = pre[rows - HALO :, :]
        act = conv * jax.nn.sigmoid(conv)
        if i < 2:
            act = act * lax.rsqrt(head_sum(act * act, blocks) + UNIT_EPS)
        act_low = act.astype(BF16)
        (q_ref, k_ref, v_ref)[i][...] = act_low
        if i == 1:
            kt_ref[...] = jnp.transpose(act_low.astype(F32)).astype(BF16)


def prep_call(seq, x, w, conv, gains, gate, pers, shift):
    rows, width = x.shape
    cols = w.shape[2]
    nb = rows // SPAN
    whole = lambda a: pl.BlockSpec(a.shape, lambda c, n=a.ndim: (0,) * n)
    row_cols = pl.BlockSpec((SPAN, cols), lambda c: (c, 0))
    return pl.pallas_call(
        functools.partial(prep_kernel, shift),
        grid=(nb,),
        in_specs=[
            pl.BlockSpec(memory_space=pltpu.SMEM),
            pl.BlockSpec((SPAN, width), lambda c: (c, 0)),
            whole(w),
            whole(conv),
            whole(gains),
            whole(gate),
            whole(pers),
        ],
        out_specs=[
            row_cols,
            row_cols,
            row_cols,
            pl.BlockSpec((cols, SPAN), lambda c: (0, c)),
            pl.BlockSpec((3, SPAN, cols), lambda c: (0, c, 0)),
            row_cols,
            pl.BlockSpec((SPAN, width), lambda c: (c, 0)),
            pl.BlockSpec((8, width), lambda c: (c, 0)),
            pl.BlockSpec((8, GATE_ROWS), lambda c: (c, 0)),
            whole(pers),
        ],
        out_shape=[
            jax.ShapeDtypeStruct((rows, cols), BF16),
            jax.ShapeDtypeStruct((rows, cols), BF16),
            jax.ShapeDtypeStruct((rows, cols), BF16),
            jax.ShapeDtypeStruct((cols, rows), BF16),
            jax.ShapeDtypeStruct((3, rows, cols), F32),
            jax.ShapeDtypeStruct((rows, cols), F32),
            jax.ShapeDtypeStruct((rows, width), BF16),
            jax.ShapeDtypeStruct((nb * 8, width), F32),
            jax.ShapeDtypeStruct((nb * 8, GATE_ROWS), F32),
            jax.ShapeDtypeStruct(pers.shape, BF16),
        ],
        scratch_shapes=[pltpu.VMEM((3, HALO + SPAN, cols), F32)],
        name="prep",
    )(seq, x, w, conv, gains, gate, pers)


def mix_kernel(block, blocks_all, shift, first, last, *refs):
    it = iter(refs)
    seq_ref, lg_ref, q_ref, k_ref, v_ref, kt_ref, pers_ref, gp_ref, a_ref, bt_ref = (
        next(it) for _ in range(10)
    )
    sa_ref, sbt_ref = (None, None) if first or last else (next(it), next(it))
    mixed_ref, tot_ref, att_ref, linv_ref = (next(it) for _ in range(4))
    if not last:
        a2_ref, bt2_ref, sa2_ref, sbt2_ref, ga_ref, gbt_ref = (next(it) for _ in range(6))
        z_ref, r_ref = next(it), next(it)
    rows, cols = q_ref.shape
    head_size = 1 << shift
    heads = cols // head_size
    a_low = a_ref[...].astype(BF16)
    bt_low = bt_ref[...].astype(BF16)
    valid, count = valid_column(seq_ref, block * rows, rows)
    weight = valid / count
    att_ref[...] = jnp.zeros((rows, cols), F32)
    linv_ref[...] = jnp.zeros((rows, cols), F32)
    tot_ref[...] = jnp.zeros((rows, cols), F32)
    if not last:
        r_ref[...] = jnp.zeros((rows, cols), F32)

    def one_head(head, carry):
        mask = head_mask(cols, shift, head)
        mask_low = mask.astype(BF16)
        ones_low = (1.0 - mask).astype(BF16)
        query = q_ref[...] * mask_low
        scaled = query * SCORE_SCALE
        raised = jnp.exp(dot_nt(scaled, pers_ref[0])).astype(BF16)
        total = dot_nn(raised, pers_ref[1] * mask_low + ones_low)
        for j in range(block + 1):
            span = slice(j * rows, (j + 1) * rows)
            raised = jnp.exp(dot_nt(scaled, k_ref[span, :]))
            if j == block:
                raised = jnp.where(
                    iota((rows, rows), 0) >= iota((rows, rows), 1), raised, 0.0
                )
            total = total + dot_nn(raised.astype(BF16), v_ref[span, :] * mask_low + ones_low)
        inverse = 1.0 / pltpu.roll(total, head_size, 1)
        inside = jnp.broadcast_to(mask, (rows, cols)) > 0.5
        linv_ref[...] = jnp.where(inside, inverse, linv_ref[...])
        attended = jnp.where(inside, total * inverse, 0.0)
        att_ref[...] = att_ref[...] + attended
        hid = dot_nn(query, a_low)
        hid = hid * jax.nn.sigmoid(hid)
        recalled = dot_nt(hid.astype(BF16), bt_low) * mask
        tot_ref[...] = tot_ref[...] + attended + recalled
        if not last:
            hid = dot_nn(k_ref[block * rows : (block + 1) * rows, :] * mask_low, a_low)
            sig = jax.nn.sigmoid(hid)
            act = (hid * sig).astype(BF16)
            z_ref[head] = act
            target = v_ref[block * rows : (block + 1) * rows, :].astype(F32)
            resid = (dot_nt(act, bt_low) - target) * mask * weight
            r_ref[...] = r_ref[...] + resid
            d_hid = dot_nn(resid.astype(BF16), bt_low) * (sig * (1.0 + hid * (1.0 - sig)))
            at = pl.ds(pl.multiple_of(head * head_size, head_size), head_size)
            ga_ref[at, :] = dot_nn(kt_ref[at, :], d_hid.astype(BF16))
        return carry

    lax.fori_loop(0, heads, one_head, 0)
    gate = jax.nn.sigmoid(gp_ref[...])
    mixed_ref[...] = (tot_ref[...] * gate).astype(BF16)
    if not last:
        resid_t = jnp.transpose(r_ref[...]).astype(BF16)
        for head in range(heads):
            at = slice(head * head_size, (head + 1) * head_size)
            gbt_ref[at, :] = dot_nn(resid_t[at, :], z_ref[head])
        width = a_ref.shape[1]
        logits = lg_ref[...]
        step = 0.2 * jax.nn.sigmoid(gate_rows(logits, 0, heads, head_size, width))
        keep = jax.nn.sigmoid(gate_rows(logits, 1, heads, head_size, width))
        stay = 1.0 - 0.5 * jax.nn.sigmoid(gate_rows(logits, 2, heads, head_size, width))
        moment_a = -step * ga_ref[...]
        moment_b = -step * gbt_ref[...]
        if not first:
            moment_a = moment_a + keep * sa_ref[...]
            moment_b = moment_b + keep * sbt_ref[...]
        sa2_ref[...] = moment_a
        sbt2_ref[...] = moment_b
        a2_ref[...] = stay * a_ref[...] + moment_a
        bt2_ref[...] = stay * bt_ref[...] + moment_b


def mix_call(block, nb, shift, seq, lg, q, k, v, kt, pers, gp, a, bt, sa, sbt):
    rows, cols = q.shape
    first, last = block == 0, block == nb - 1
    heads = cols >> shift
    whole = lambda s: pl.BlockSpec(s, lambda i, n=len(s): (0,) * n)
    at_block = pl.BlockSpec((SPAN, cols), lambda i: (block, 0))
    upto = pl.BlockSpec(((block + 1) * SPAN, cols), lambda i: (0, 0))
    state = whole(a.shape)
    ins = [seq, lg, q, k, v, kt, pers, gp, a, bt]
    in_specs = [
        pl.BlockSpec(memory_space=pltpu.SMEM),
        pl.BlockSpec((8, GATE_ROWS), lambda i: (block, 0)),
        at_block,
        upto,
        upto,
        pl.BlockSpec((cols, SPAN), lambda i: (0, block)),
        whole(pers.shape),
        at_block,
        state,
        state,
    ]
    if not (first or last):
        ins += [sa, sbt]
        in_specs += [state, state]
    row_spec = whole((SPAN, cols))
    outs = [jax.ShapeDtypeStruct((SPAN, cols), BF16)] + [
        jax.ShapeDtypeStruct((SPAN, cols), F32)
    ] * 3
    out_specs = [row_spec] * 4
    scratch = []
    if not last:
        outs += [jax.ShapeDtypeStruct(a.shape, F32)] * 6
        out_specs += [state] * 6
        scratch = [pltpu.VMEM((heads, SPAN, a.shape[1]), BF16), pltpu.VMEM((SPAN, cols), F32)]
    return pl.pallas_call(
        functools.partial(mix_kernel, block, nb, shift, first, last),
        grid=(1,),
        in_specs=in_specs,
        out_specs=out_specs,
        out_shape=outs,
        scratch_shapes=scratch,
        name=f"mix_{block}",
    )(*ins)


def ffn_kernel(
    peer_ref,
    x_ref,
    m0_ref,
    m1_ref,
    m2_ref,
    m3_ref,
    ow_ref,
    gain_ref,
    fin_ref,
    fout_ref,
    cot_ref,
    res_ref,
    nt_ref,
    hid_ref,
    dgu_ref,
    part_keep_ref,
    part_send_ref,
    dn_keep_ref,
    dn_send_ref,
    gg_ref,
    part_ref,
):
    rows, width = x_ref.shape
    cols = m0_ref.shape[1]
    shards = width // cols
    branch = None
    for j, m_ref in enumerate((m0_ref, m1_ref, m2_ref, m3_ref)):
        at = pl.ds(pl.multiple_of(peer_ref[j] * cols, cols), cols)
        weight = jnp.concatenate([ow_ref[p, at, :] for p in range(shards)], 1)
        term = dot_nn(m_ref[...], weight)
        branch = term if branch is None else branch + term
    residual = x_ref[...].astype(F32) + branch
    res_ref[...] = residual
    scale = lax.rsqrt(jnp.mean(residual * residual, -1, keepdims=True) + NORM_EPS)
    low = (residual * scale * gain_ref[1:2, :]).astype(BF16)
    nt_ref[...] = low
    gate_pre = dot_nn(low, fin_ref[0])
    up_pre = dot_nn(low, fin_ref[1])
    sig = jax.nn.sigmoid(gate_pre)
    silu = gate_pre * sig
    hidden = (silu * up_pre).astype(BF16)
    hid_ref[...] = hidden
    cot = jnp.concatenate([cot_ref[p] for p in range(shards)], 1)
    d_hidden = dot_nt(cot, fout_ref[...])
    slope = sig * (1.0 + gate_pre * (1.0 - sig))
    d_gate = (d_hidden * up_pre * slope).astype(BF16)
    d_up = (d_hidden * silu).astype(BF16)
    dgu_ref[0] = d_gate
    dgu_ref[1] = d_up
    d_normed = dot_nt(d_gate, fin_ref[0]) + dot_nt(d_up, fin_ref[1])
    gains = jnp.sum(d_normed * residual * scale, 0, keepdims=True)

    @pl.when(pl.program_id(0) == 0)
    def _():
        gg_ref[...] = jnp.zeros_like(gg_ref)

    gg_ref[...] = gg_ref[...] + jnp.broadcast_to(gains, gg_ref.shape)
    half = width // 2
    part_ref[...] = d_normed.astype(BF16)
    core = peer_ref[0] & 1
    dn_keep_ref[...] = part_ref[:, pl.ds(pl.multiple_of(core * half, half), half)]
    dn_send_ref[...] = part_ref[:, pl.ds(pl.multiple_of((1 - core) * half, half), half)]
    part_ref[...] = dot_nn(hidden, fout_ref[...]).astype(BF16)
    for slot, out_ref in ((0, part_keep_ref), (1, part_send_ref)):
        for n in range(2):
            start = pl.multiple_of(peer_ref[slot + 2 * n] * cols, cols)
            out_ref[n] = part_ref[:, pl.ds(start, cols)]


def ffn_call(block, peers, x, mixed, ow, gains, fin, fout, cot):
    width = x.shape[1]
    cols = mixed[0].shape[1]
    tile = SPAN // 2
    steps = SPAN // tile
    shards = width // cols
    hidden = fout.shape[0]
    whole = lambda a: pl.BlockSpec(a.shape, lambda i, n=a.ndim: (0,) * n)
    row = lambda n: pl.BlockSpec((tile, n), lambda i: (i, 0))
    stacked = lambda n, w: pl.BlockSpec((n, tile, w), lambda i: (0, i, 0))
    struct = jax.ShapeDtypeStruct
    return pl.pallas_call(
        ffn_kernel,
        grid=(steps,),
        in_specs=[
            pl.BlockSpec(memory_space=pltpu.SMEM),
            pl.BlockSpec((tile, width), lambda i: (block * steps + i, 0)),
            row(cols),
            row(cols),
            row(cols),
            row(cols),
            whole(ow),
            whole(gains),
            whole(fin),
            whole(fout),
            pl.BlockSpec((shards, tile, cols), lambda i: (0, block * steps + i, 0)),
        ],
        out_specs=[
            row(width),
            row(width),
            row(hidden),
            stacked(2, hidden),
            stacked(2, cols),
            stacked(2, cols),
            row(width // 2),
            row(width // 2),
            pl.BlockSpec((8, width), lambda i: (0, 0)),
        ],
        out_shape=[
            struct((SPAN, width), F32),
            struct((SPAN, width), BF16),
            struct((SPAN, hidden), BF16),
            struct((2, SPAN, hidden), BF16),
            struct((2, SPAN, cols), BF16),
            struct((2, SPAN, cols), BF16),
            struct((SPAN, width // 2), BF16),
            struct((SPAN, width // 2), BF16),
            struct((8, width), F32),
        ],
        scratch_shapes=[pltpu.VMEM((tile, width), BF16)],
        name=f"ffn_{block}",
    )(peers, x, *mixed, ow, gains, fin, fout, cot)


def turn_kernel(
    peer_ref,
    s1_ref,
    r2_ref,
    ps1_ref,
    pr2_ref,
    res_ref,
    cot_ref,
    ow_ref,
    gain_ref,
    gp_ref,
    tot_ref,
    dres_ref,
    rescol_ref,
    dbr_ref,
    dga_ref,
    dgp_ref,
    full_ref,
):
    rows, width = res_ref.shape
    cols = gp_ref.shape[1]
    shards = width // cols
    half = width // 2
    core = peer_ref[0] & 1
    at_own = pl.ds(pl.multiple_of(core * half, half), half)
    at_other = pl.ds(pl.multiple_of((1 - core) * half, half), half)
    full_ref[:, at_own] = s1_ref[...].astype(F32) + r2_ref[...].astype(F32)
    full_ref[:, at_other] = ps1_ref[...].astype(F32) + pr2_ref[...].astype(F32)
    residual = res_ref[...]
    scale = lax.rsqrt(jnp.mean(residual * residual, -1, keepdims=True) + NORM_EPS)
    gained = full_ref[...] * gain_ref[1:2, :]
    inner = jnp.sum(gained * residual, -1, keepdims=True) / width
    cot = jnp.concatenate([cot_ref[p].astype(F32) for p in range(shards)], 1)
    d_residual = cot + scale * gained - residual * (scale * scale * scale * inner)
    d_branch = d_residual.astype(BF16)
    own = pl.ds(pl.multiple_of(peer_ref[0] * cols, cols), cols)
    weight = jnp.concatenate([ow_ref[p, own, :] for p in range(shards)], 1)
    d_mixed = dot_nt(d_branch, weight)
    full_ref[...] = d_residual
    mine = full_ref[:, own]
    dres_ref[...] = mine
    dbr_ref[...] = mine.astype(BF16)
    rescol_ref[...] = res_ref[:, own]
    gate = jax.nn.sigmoid(gp_ref[...])
    d_gated = d_mixed * gate
    dga_ref[...] = d_gated.astype(BF16)
    dgp_ref[...] = (d_gated * tot_ref[...] * (1.0 - gate)).astype(BF16)


def turn_call(block, peers, pieces, res, cot, ow, gains, gp, tot):
    width = res.shape[1]
    cols = gp.shape[1]
    tile = SPAN // 2
    steps = SPAN // tile
    shards = width // cols
    whole = lambda a: pl.BlockSpec(a.shape, lambda i, n=a.ndim: (0,) * n)
    row = lambda n: pl.BlockSpec((tile, n), lambda i: (i, 0))
    struct = jax.ShapeDtypeStruct
    return pl.pallas_call(
        turn_kernel,
        grid=(steps,),
        in_specs=[
            pl.BlockSpec(memory_space=pltpu.SMEM),
            row(width // 2),
            row(width // 2),
            row(width // 2),
            row(width // 2),
            row(width),
            pl.BlockSpec((shards, tile, cols), lambda i: (0, block * steps + i, 0)),
            whole(ow),
            whole(gains),
            pl.BlockSpec((tile, cols), lambda i: (block * steps + i, 0)),
            row(cols),
        ],
        out_specs=[row(cols)] * 5,
        out_shape=[
            struct((SPAN, cols), F32),
            struct((SPAN, cols), F32),
            struct((SPAN, cols), BF16),
            struct((SPAN, cols), BF16),
            struct((SPAN, cols), BF16),
        ],
        scratch_shapes=[pltpu.VMEM((tile, width), F32)],
        name=f"turn_{block}",
    )(peers, *pieces, res, cot, ow, gains, gp, tot)


def back_kernel(block, nb, shift, *refs):
    it = iter(refs)
    take = lambda n: [next(it) for _ in range(n)]
    first, last = block == 0, block == nb - 1
    seq_ref, q_ref, k_ref, v_ref, kt_ref, pers_ref, dga_ref, att_ref, linv_ref = take(9)
    a_ref, bt_ref = take(2)
    if not last:
        dk_in_ref, dv_in_ref, dp_in_ref, lg_ref, ga_ref, gbt_ref, ab_in_ref, btb_in_ref = take(8)
        sab_in_ref, sbtb_in_ref = take(2) if block < nb - 2 else (None, None)
        sa_ref, sbt_ref = (None, None) if first else take(2)
    dq_ref, dk_ref, dv_ref, dp_ref, ab_ref, btb_ref = take(6)
    if not last:
        (dlg_ref,) = take(1)
        sab_ref, sbtb_ref = (None, None) if first else take(2)
    lt_ref, dt_ref, dqt_ref, qt_ref, dot_ref = take(5)
    if not last:
        z_ref, zd_ref, r_ref, y_ref, h_ref = take(5)
    rows, cols = q_ref.shape
    head_size = 1 << shift
    heads = cols // head_size
    own = slice(block * rows, (block + 1) * rows)
    a_low = a_ref[...].astype(BF16)
    bt_low = bt_ref[...].astype(BF16)
    if last:
        dk_ref[...] = jnp.zeros(dk_ref.shape, F32)
        dv_ref[...] = jnp.zeros(dv_ref.shape, F32)
        dp_ref[...] = jnp.zeros(dp_ref.shape, F32)
        ab_ref[...] = jnp.zeros(ab_ref.shape, F32)
        btb_ref[...] = jnp.zeros(btb_ref.shape, F32)
    else:
        dk_ref[...] = dk_in_ref[...]
        dv_ref[...] = dv_in_ref[...]
        dp_ref[...] = dp_in_ref[...]
    pick = (iota((8, cols), 1) >> shift) == iota((8, cols), 0)
    start = iota((8, cols), 1) == (iota((8, cols), 0) << shift)
    lt_ref[...] = dot_nt(jnp.where(start, 1.0, 0.0), linv_ref[...], HIGH)
    d_gated = dga_ref[...].astype(F32)
    dt_ref[...] = dot_nt(jnp.where(pick, 1.0, 0.0), d_gated * att_ref[...], HIGH)
    dq_ref[...] = jnp.zeros((rows, cols), F32)
    qt_ref[...] = jnp.transpose(q_ref[...].astype(F32)).astype(BF16)
    dot_ref[...] = jnp.transpose(d_gated).astype(BF16)
    if not last:
        valid, count = valid_column(seq_ref, block * rows, rows)
        weight = valid / count
        width = a_ref.shape[1]
        logits = lg_ref[...]
        sig_step = jax.nn.sigmoid(gate_rows(logits, 0, heads, head_size, width))
        keep = jax.nn.sigmoid(gate_rows(logits, 1, heads, head_size, width))
        sig_forget = jax.nn.sigmoid(gate_rows(logits, 2, heads, head_size, width))
        tot_a, tot_b = ab_in_ref[...], btb_in_ref[...]
        if sab_in_ref is not None:
            tot_a, tot_b = tot_a + sab_in_ref[...], tot_b + sbtb_in_ref[...]
        h_ref[0] = (-0.2 * sig_step * tot_a).astype(BF16)
        h_ref[1] = (-0.2 * sig_step * tot_b).astype(BF16)
        d_step = -(ga_ref[...] * tot_a + gbt_ref[...] * tot_b)
        groups = [d_step * (0.2 * sig_step * (1.0 - sig_step)), None, None]
        if not first:
            groups[1] = (sa_ref[...] * tot_a + sbt_ref[...] * tot_b) * (keep * (1.0 - keep))
        d_forget = -(a_ref[...] * ab_in_ref[...] + bt_ref[...] * btb_in_ref[...])
        groups[2] = d_forget * (0.5 * sig_forget * (1.0 - sig_forget))
        d_logits = jnp.zeros((8, GATE_ROWS), F32)
        for g, value in enumerate(groups):
            if value is None:
                continue
            for head in range(heads):
                part = value[head * head_size : (head + 1) * head_size, :]
                figure = jnp.sum(jnp.sum(part, 1, keepdims=True), 0, keepdims=True)
                here = iota((8, GATE_ROWS), 1) == g * heads + head
                d_logits = d_logits + jnp.where(here, 1.0, 0.0) * figure
        dlg_ref[...] = d_logits
        stay = 1.0 - 0.5 * sig_forget
        ab_ref[...] = stay * ab_in_ref[...]
        btb_ref[...] = stay * btb_in_ref[...]
        if not first:
            sab_ref[...] = keep * tot_a
            sbtb_ref[...] = keep * tot_b
        r_ref[...] = jnp.zeros((rows, cols), F32)
        y_ref[...] = jnp.zeros((rows, cols), F32)

    def one_head(head, carry):
        mask = head_mask(cols, shift, head)
        mask_low = mask.astype(BF16)
        query = q_ref[...] * mask_low
        scaled = query * SCORE_SCALE
        d_out = dga_ref[...] * mask_low
        at = pl.ds(pl.multiple_of(head * head_size, head_size), head_size)
        inverse = lt_ref[pl.ds(head, 1), :]
        delta = dt_ref[pl.ds(head, 1), :]
        probs = jnp.exp(dot_nt(pers_ref[0], scaled)) * inverse
        d_scores = (probs * (dot_nt(pers_ref[1], d_out) - delta)).astype(BF16)
        dp_ref[0] = dp_ref[0] + dot_nn(d_scores, scaled)
        dp_ref[1] = dp_ref[1] + dot_nn(probs.astype(BF16), d_out)
        d_query = lax.dot_general(
            d_scores, pers_ref[0], (((0,), (0,)), ((), ())), preferred_element_type=F32
        )
        d_query = d_query * SCORE_SCALE
        d_query_t = jnp.zeros((head_size, rows), F32)
        for j in range(block + 1):
            span = slice(j * rows, (j + 1) * rows)
            probs = jnp.exp(dot_nt(k_ref[span, :], scaled)) * inverse
            if j == block:
                probs = jnp.where(iota((rows, rows), 0) <= iota((rows, rows), 1), probs, 0.0)
            d_scores = (probs * (dot_nt(v_ref[span, :], d_out) - delta)).astype(BF16)
            dv_ref[span, :] = dv_ref[span, :] + dot_nn(probs.astype(BF16), d_out)
            dk_ref[span, :] = dk_ref[span, :] + dot_nn(d_scores, scaled)
            d_query_t = d_query_t + dot_nn(kt_ref[at, span], d_scores)
        dqt_ref[at, :] = d_query_t * SCORE_SCALE
        hid = dot_nn(query, a_low)
        sig = jax.nn.sigmoid(hid)
        d_hid = dot_nn(d_out, bt_low) * (sig * (1.0 + hid * (1.0 - sig)))
        d_hid = d_hid.astype(BF16)
        dq_ref[...] = dq_ref[...] + (d_query + dot_nt(d_hid, a_low)) * mask
        grad_a = dot_nn(qt_ref[at, :], d_hid)
        grad_b = dot_nn(dot_ref[at, :], (hid * sig).astype(BF16))
        if not last:
            key = k_ref[own, :] * mask_low
            hid = dot_nn(key, a_low)
            probe = dot_nn(key, h_ref[0])
            sig = jax.nn.sigmoid(hid)
            act = (hid * sig).astype(BF16)
            z_ref[head] = act
            slope = sig * (1.0 + hid * (1.0 - sig))
            curve = sig * (1.0 - sig) * (2.0 + hid * (1.0 - 2.0 * sig))
            target = v_ref[own, :].astype(F32)
            resid = (dot_nt(act, bt_low) - target) * mask * weight
            r_ref[...] = r_ref[...] + resid
            resid = resid.astype(BF16)
            d_act = dot_nn(resid, bt_low)
            d_slope = (probe * slope).astype(BF16)
            zd_ref[head] = d_slope
            d_net = (dot_nt(act, h_ref[1]) + dot_nt(d_slope, bt_low)) * mask * weight
            y_ref[...] = y_ref[...] + d_net
            back = dot_nn(resid, h_ref[1]) + dot_nn(d_net.astype(BF16), bt_low)
            d_hid = (probe * d_act * curve + back * slope).astype(BF16)
            direct = (d_act * slope).astype(BF16)
            d_key = (dot_nt(direct, h_ref[0]) + dot_nt(d_hid, a_low)) * mask
            dk_ref[own, :] = dk_ref[own, :] + d_key
            grad_a = grad_a + dot_nn(kt_ref[at, own], d_hid)
        ab_ref[at, :] = ab_ref[at, :] + grad_a
        btb_ref[at, :] = btb_ref[at, :] + grad_b
        return carry

    lax.fori_loop(0, heads, one_head, 0)
    dq_ref[...] = dq_ref[...] + jnp.transpose(dqt_ref[...])
    if not last:
        dv_ref[own, :] = dv_ref[own, :] - y_ref[...]
        resid_t = jnp.transpose(r_ref[...]).astype(BF16)
        net_t = jnp.transpose(y_ref[...]).astype(BF16)
        for head in range(heads):
            at = slice(head * head_size, (head + 1) * head_size)
            grad_b = dot_nn(resid_t[at, :], zd_ref[head]) + dot_nn(net_t[at, :], z_ref[head])
            btb_ref[at, :] = btb_ref[at, :] + grad_b


def back_call(block, nb, shift, seq, q, k, v, kt, pers, dga, att, linv, state, grads, adjoint):
    cols = q.shape[1]
    heads = cols >> shift
    first, last = block == 0, block == nb - 1
    done = (block + 1) * SPAN
    whole = lambda s: pl.BlockSpec(s, lambda i, n=len(s): (0,) * n)
    at_block = pl.BlockSpec((SPAN, cols), lambda i: (block, 0))
    upto = pl.BlockSpec((done, cols), lambda i: (0, 0))
    rows_spec = whole((SPAN, cols))
    square = state["a"].shape
    ins = [seq, q, k, v, kt, pers, dga, att, linv, state["a"], state["bt"]]
    in_specs = [
        pl.BlockSpec(memory_space=pltpu.SMEM),
        at_block,
        upto,
        upto,
        pl.BlockSpec((cols, done), lambda i: (0, 0)),
        whole(pers.shape),
        rows_spec,
        rows_spec,
        rows_spec,
        whole(square),
        whole(square),
    ]
    if not last:
        ins += [grads["dk"], grads["dv"], grads["dp"], state["lg"], state["ga"], state["gbt"]]
        ins += [adjoint["ab"], adjoint["btb"]]
        in_specs += [upto, upto, whole(pers.shape)]
        in_specs += [pl.BlockSpec((8, GATE_ROWS), lambda i: (block, 0))]
        in_specs += [whole(square)] * 4
        if block < nb - 2:
            ins += [adjoint["sab"], adjoint["sbtb"]]
            in_specs += [whole(square)] * 2
        if not first:
            ins += [state["sa"], state["sbt"]]
            in_specs += [whole(square)] * 2
    names = ["dq", "dk", "dv", "dp", "ab", "btb"]
    shapes = [(SPAN, cols), (done, cols), (done, cols), pers.shape, square, square]
    if not last:
        names.append("dlg")
        shapes.append((8, GATE_ROWS))
        if not first:
            names += ["sab", "sbtb"]
            shapes += [square, square]
    scratch = [
        pltpu.VMEM((8, SPAN), F32),
        pltpu.VMEM((8, SPAN), F32),
        pltpu.VMEM((cols, SPAN), F32),
        pltpu.VMEM((cols, SPAN), BF16),
        pltpu.VMEM((cols, SPAN), BF16),
    ]
    if not last:
        scratch += [
            pltpu.VMEM((heads, SPAN, square[1]), BF16),
            pltpu.VMEM((heads, SPAN, square[1]), BF16),
            pltpu.VMEM((SPAN, cols), F32),
            pltpu.VMEM((SPAN, cols), F32),
            pltpu.VMEM((2,) + square, BF16),
        ]
    outs = pl.pallas_call(
        functools.partial(back_kernel, block, nb, shift),
        grid=(1,),
        in_specs=in_specs,
        out_specs=[whole(s) for s in shapes],
        out_shape=[jax.ShapeDtypeStruct(s, F32) for s in shapes],
        scratch_shapes=scratch,
        name=f"back_{block}",
    )(*ins)
    return dict(zip(names, outs))


def unprep_kernel(block, nb, shift, *refs):
    it = iter(refs)
    take = lambda n: [next(it) for _ in range(n)]
    first, last = block == 0, block == nb - 1
    seq_ref, peer_ref, dq_ref, dk_ref, dv_ref, dgp_ref, pre_ref, w_ref, conv_ref = take(9)
    x_ref, gain_ref = take(2)
    (halo_ref,) = (None,) if first else take(1)
    next_ref, dlg_ref, gate_ref = (None, None, None) if last else take(3)
    dproj_ref, keep_ref, send_ref, inner_ref, cg_ref, gg_ref, edge_ref = take(7)
    ext_ref, dext_ref, low_ref = take(3)
    rows, cols = dq_ref.shape
    width = x_ref.shape[1]
    blocks = head_blocks(cols, shift)
    taps = conv_ref.shape[1]
    d_normed = dot_nt(dgp_ref[...], w_ref[3])
    dproj_ref[3] = dgp_ref[...]
    cg_ref[...] = jnp.zeros(cg_ref.shape, F32)
    for i in range(3):
        pre = pre_ref[i]
        ext_ref[0:HALO, :] = jnp.zeros((HALO, cols), F32) if first else halo_ref[i]
        ext_ref[HALO : HALO + rows, :] = pre
        shifted = [pre] + [ext_ref[HALO - j : HALO - j + rows, :] for j in range(1, taps)]
        conv = conv_ref[i, 0:1, :] * pre
        for j in range(1, taps):
            conv = conv + conv_ref[i, j : j + 1, :] * shifted[j]
        sig = jax.nn.sigmoid(conv)
        d_act = (dq_ref, dk_ref, dv_ref)[i][...]
        if i < 2:
            act = conv * sig
            scale = lax.rsqrt(head_sum(act * act, blocks) + UNIT_EPS)
            d_act = scale * (d_act - act * (scale * scale * head_sum(d_act * act, blocks)))
        d_conv = d_act * (sig * (1.0 + conv * (1.0 - sig)))
        edge_ref[i] = d_conv[0:HALO, :]
        dext_ref[0:rows, :] = d_conv
        dext_ref[rows : rows + HALO, :] = (
            jnp.zeros((HALO, cols), F32) if last else next_ref[i]
        )
        d_pre = conv_ref[i, 0:1, :] * d_conv
        for j in range(taps):
            if j:
                d_pre = d_pre + conv_ref[i, j : j + 1, :] * dext_ref[j : j + rows, :]
            cg_ref[i * taps + j : i * taps + j + 1, :] = jnp.sum(
                d_conv * shifted[j], 0, keepdims=True
            )
        d_low = d_pre.astype(BF16)
        dproj_ref[i] = d_low
        d_normed = d_normed + dot_nt(d_low, w_ref[i])
    if not last:
        valid, count = valid_column(seq_ref, block * rows, rows)
        d_mean = jnp.dot(
            dlg_ref[...], gate_ref[...], preferred_element_type=F32, precision=HIGH
        )
        d_normed = d_normed + (valid / count) * d_mean[0:1, :]
    x = x_ref[...].astype(F32)
    scale = lax.rsqrt(jnp.mean(x * x, -1, keepdims=True) + NORM_EPS)
    weighted = d_normed * x
    gg_ref[...] = jnp.broadcast_to(jnp.sum(weighted * scale, 0, keepdims=True), gg_ref.shape)
    ones = jnp.ones((8, width), BF16)
    high, rest = two_parts(weighted * gain_ref[0:1, :])
    inner_ref[...] = dot_nt(ones, high) + dot_nt(ones, rest)
    low_ref[...] = d_normed.astype(BF16)
    for slot, out_ref in ((0, keep_ref), (1, send_ref)):
        for n in range(2):
            start = pl.multiple_of(peer_ref[slot + 2 * n] * cols, cols)
            out_ref[n] = low_ref[:, pl.ds(start, cols)]


def unprep_call(block, nb, shift, seq, peers, back, dgp, pre, w, conv, x, gains, edge, gate):
    cols = dgp.shape[1]
    width = x.shape[1]
    first, last = block == 0, block == nb - 1
    whole = lambda a: pl.BlockSpec(a.shape, lambda i, n=a.ndim: (0,) * n)
    smem = pl.BlockSpec(memory_space=pltpu.SMEM)
    at_block = pl.BlockSpec((SPAN, cols), lambda i: (block, 0))
    ins = [seq, peers, back["dq"], back["dk"], back["dv"], dgp, pre, w, conv, x, gains]
    in_specs = [
        smem,
        smem,
        whole(back["dq"]),
        at_block,
        at_block,
        whole(dgp),
        pl.BlockSpec((3, SPAN, cols), lambda i: (0, block, 0)),
        whole(w),
        whole(conv),
        pl.BlockSpec((SPAN, width), lambda i: (block, 0)),
        whole(gains),
    ]
    if not first:
        ins.append(pre)
        in_specs.append(
            pl.BlockSpec((3, HALO, cols), lambda i: (0, block * (SPAN // HALO) - 1, 0))
        )
    if not last:
        ins += [edge, back["dlg"], gate]
        in_specs += [whole(edge), whole(back["dlg"]), whole(gate)]
    struct = jax.ShapeDtypeStruct
    outs = [
        struct((4, SPAN, cols), BF16),
        struct((2, SPAN, cols), BF16),
        struct((2, SPAN, cols), BF16),
        struct((8, SPAN), F32),
        struct((16, cols), F32),
        struct((8, width), F32),
        struct((3, HALO, cols), F32),
    ]
    names = ["dproj", "keep", "send", "inner", "cg", "gg", "edge"]
    got = pl.pallas_call(
        functools.partial(unprep_kernel, block, nb, shift),
        grid=(1,),
        in_specs=in_specs,
        out_specs=[pl.BlockSpec(s.shape, lambda i, n=len(s.shape): (0,) * n) for s in outs],
        out_shape=outs,
        scratch_shapes=[
            pltpu.VMEM((HALO + SPAN, cols), F32),
            pltpu.VMEM((SPAN + HALO, cols), F32),
            pltpu.VMEM((SPAN, width), BF16),
        ],
        name=f"unprep_{block}",
    )(*ins)
    return dict(zip(names, got))


def per_device(
    layer_input,
    proj_weight,
    conv_weight,
    persist_kv,
    memory_in,
    memory_out,
    memory_gate,
    out_weight,
    ffn_in,
    ffn_out,
    norm_gains,
    seq_len,
    out_grad,
):
    rows, width = layer_input.shape
    cols = proj_weight.shape[2]
    heads = persist_kv.shape[1]
    head_size = persist_kv.shape[3]
    shift = head_size.bit_length() - 1
    mem_hid = memory_in.shape[2]
    nb = rows // SPAN
    taps = conv_weight.shape[1]
    me = lax.axis_index("head")
    count = width // cols
    peers = jnp.stack([me, me ^ 1, me ^ 2, me ^ 3]).astype(jnp.int32)
    swap = lambda a, bit: lax.ppermute(a, "head", [(i, i ^ bit) for i in range(count)])
    ow = lax.all_gather(out_weight, "head", axis=0, tiled=False)
    cot = lax.all_gather(out_grad, "head", axis=0, tiled=False)
    gate = jnp.transpose(memory_gate, (1, 2, 0)).reshape(3 * heads, width)
    gate = jnp.pad(gate, ((0, GATE_ROWS - 3 * heads), (0, 0)))
    pers = jnp.transpose(persist_kv, (0, 2, 1, 3)).reshape(2, -1, cols)
    q, k, v, kt, pre, gp, nl, mean, lg, pers_low = prep_call(
        seq_len, layer_input, proj_weight, conv_weight, norm_gains, gate, pers, shift
    )
    a = memory_in.reshape(cols, mem_hid)
    bt = jnp.transpose(memory_out, (0, 2, 1)).reshape(cols, mem_hid)
    sa = sbt = None
    states, mixes = [], []
    for c in range(nb):
        state = dict(a=a, bt=bt, sa=sa, sbt=sbt, lg=lg)
        got = mix_call(c, nb, shift, seq_len, lg, q, k, v, kt, pers_low, gp, a, bt, sa, sbt)
        if c < nb - 1:
            a, bt, sa, sbt, state["ga"], state["gbt"] = got[4:]
        states.append(state)
        mixes.append(dict(mixed=got[0], tot=got[1], att=got[2], linv=got[3]))
    for mix in mixes:
        near, far = swap(mix["mixed"], 1), swap(mix["mixed"], 2)
        mix["all"] = (mix["mixed"], near, far, swap(far, 1))
    names = ["res", "nt", "hid", "dgu", "pkeep", "psend", "dkeep", "dsend", "gg"]
    ffns = []
    for c in range(nb):
        got = ffn_call(
            c, peers, layer_input, mixes[c]["all"], ow, norm_gains, ffn_in, ffn_out, cot
        )
        ffn = dict(zip(names, got))
        s1 = (ffn["dkeep"].astype(F32) + swap(ffn["dsend"], 1).astype(F32)).astype(BF16)
        r2 = swap(s1, 2)
        ffn["pieces"] = (s1, r2, swap(s1, 1), swap(r2, 1))
        part = (ffn["pkeep"].astype(F32) + swap(ffn["psend"], 1).astype(F32)).astype(BF16)
        ffn["out"] = part[0].astype(F32) + swap(part[1], 2).astype(F32)
        ffns.append(ffn)
    rows_of = lambda key, axis: jnp.concatenate([f[key] for f in ffns], axis)
    normed_two, hidden, dgu = rows_of("nt", 0), rows_of("hid", 0), rows_of("dgu", 1)
    cot_full = jnp.transpose(cot, (1, 0, 2)).reshape(rows, width)
    along_rows = (((0,), (0,)), ((), ()))
    ffn_out_grad = lax.dot_general(hidden, cot_full, along_rows, preferred_element_type=F32)
    ffn_in_grad = [
        lax.dot_general(normed_two, dgu[i], along_rows, preferred_element_type=F32)
        for i in range(2)
    ]
    ffn_grads = lax.psum(
        jnp.stack([ffn_in_grad[0], ffn_in_grad[1], ffn_out_grad]).astype(BF16), "dp"
    )
    grads = adjoint = edge = None
    turns, unpreps, dlgs = [None] * nb, [None] * nb, [None] * nb
    for c in reversed(range(nb)):
        dres, rescol, dbr, dga, dgp = turn_call(
            c, peers, ffns[c]["pieces"], ffns[c]["res"], cot, ow, norm_gains, gp, mixes[c]["tot"]
        )
        turns[c] = dict(dres=dres, rescol=rescol, dbr=dbr)
        back = back_call(
            c, nb, shift, seq_len, q, k, v, kt, pers_low, dga, mixes[c]["att"], mixes[c]["linv"],
            states[c], grads, adjoint,
        )
        grads = adjoint = back
        dlgs[c] = back.get("dlg")
        unpreps[c] = unprep_call(
            c, nb, shift, seq_len, peers, back, dgp, pre, proj_weight, conv_weight, layer_input,
            norm_gains, edge, gate,
        )
        edge = unpreps[c]["edge"]
    layer_output = jnp.concatenate(
        [(turns[c]["rescol"] + ffns[c]["out"]).astype(BF16) for c in range(nb)], 0
    )
    own_gain = lax.dynamic_slice_in_dim(norm_gains[0:1], me * cols, cols, 1)
    d_inputs = []
    for c in range(nb):
        up = unpreps[c]
        half = (up["keep"].astype(F32) + swap(up["send"], 1).astype(F32)).astype(BF16)
        d_normed = half[0].astype(F32) + swap(half[1], 2).astype(F32)
        inner = up["inner"]
        inner = inner + swap(inner, 1)
        inner = (inner + swap(inner, 2))[0][:, None]
        x = layer_input[c * SPAN : (c + 1) * SPAN].astype(F32)
        scale = lax.rsqrt(jnp.mean(x * x, -1, keepdims=True) + NORM_EPS)
        x_own = lax.dynamic_slice_in_dim(x, me * cols, cols, 1)
        d_one = scale * own_gain * d_normed - x_own * (scale * scale * scale * inner / width)
        d_inputs.append(turns[c]["dres"] + d_one)
    input_grad = jnp.concatenate(d_inputs, 0)
    dproj = jnp.concatenate([u["dproj"] for u in unpreps], 1)
    proj_grad = jnp.stack(
        [
            lax.dot_general(nl, dproj[i], along_rows, preferred_element_type=F32)
            for i in range(4)
        ]
    ).astype(BF16)
    dbr = jnp.concatenate([t["dbr"] for t in turns], 0)
    out_grads = jnp.zeros((width, cols), BF16)
    for j in range(4):
        piece = jnp.concatenate([m["all"][j] for m in mixes], 0)
        part = lax.dot_general(piece, dbr, along_rows, preferred_element_type=F32)
        out_grads = lax.dynamic_update_slice(out_grads, part.astype(BF16), (peers[j] * cols, 0))
    conv_grad = sum(u["cg"] for u in unpreps)[: 3 * taps]
    keys = pers[0].reshape(-1, heads, head_size)
    d_keys = grads["dp"][0].reshape(keys.shape)
    unit = lax.rsqrt(jnp.sum(keys * keys, -1, keepdims=True) + UNIT_EPS)
    d_keys = unit * (
        d_keys - keys * (unit * unit * jnp.sum(d_keys * keys, -1, keepdims=True))
    )
    d_pers = jnp.stack([d_keys.reshape(-1, cols), grads["dp"][1]])
    gate_grad = jnp.zeros((3 * heads, width), F32)
    for c in range(nb - 1):
        gate_grad = gate_grad + dlgs[c][0, : 3 * heads, None] * mean[8 * c][None, :]
    gains = jnp.stack(
        [sum(u["gg"][0] for u in unpreps), sum(f["gg"][0] for f in ffns)]
    )
    gains = gains + swap(gains, 1)
    gains = gains + swap(gains, 2)
    tail = [
        proj_grad,
        out_grads,
        grads["ab"].astype(BF16),
        grads["btb"].astype(BF16),
    ]
    small = jnp.concatenate(
        [g.reshape(-1, cols) for g in (gate_grad, conv_grad, d_pers, gains)], 0
    )
    tail = lax.psum(tail, "dp")
    small = lax.psum(small, "dp")
    sizes = [3 * heads * width, 3 * taps * cols, d_pers.size, 2 * width]
    cuts = [0]
    for size in sizes:
        cuts.append(cuts[-1] + size // cols)
    gate_grad, conv_grad, d_pers, gains = (small[b:e] for b, e in zip(cuts, cuts[1:]))
    return (
        layer_output,
        input_grad,
        tail[0].astype(F32),
        conv_grad.reshape(3, taps, cols),
        jnp.transpose(d_pers.reshape(2, -1, heads, head_size), (0, 2, 1, 3)),
        tail[2].astype(F32).reshape(memory_in.shape),
        jnp.transpose(tail[3].astype(F32).reshape(heads, head_size, mem_hid), (0, 2, 1)),
        jnp.transpose(gate_grad.reshape(3, heads, width), (2, 0, 1)),
        tail[1].astype(F32),
        ffn_grads[:2].astype(F32),
        ffn_grads[2].astype(F32),
        gains.reshape(2, width),
    )


def solution(mesh):
    in_specs = (
        P("dp", None),
        P(None, None, "head"),
        P(None, None, "head"),
        P(None, "head", None, None),
        P("head", None, None),
        P("head", None, None),
        P(None, None, "head"),
        P(None, "head"),
        P(None, None, "head"),
        P("head", None),
        P(),
        P("dp"),
        P("dp", "head"),
    )
    out_specs = (
        P("dp", "head"),
        P("dp", "head"),
        P(None, None, "head"),
        P(None, None, "head"),
        P(None, "head", None, None),
        P("head", None, None),
        P("head", None, None),
        P(None, None, "head"),
        P(None, "head"),
        P(None, None, "head"),
        P("head", None),
        P(),
    )
    return jax.shard_map(
        per_device, mesh=mesh, in_specs=in_specs, out_specs=out_specs, check_vma=False
    )
```

time: 1940 us -> 734 us (0.38)
  waiting for transfers between devices: 974 us -> 388 us
  matrix products: 477 us -> 24.1 us
  local copies, waits for them, and re-layouts: 263 us -> 48.2 us
  Pallas kernels: 0 us -> 186 us
  other arithmetic: 178 us -> 41.7 us
  loops' own time: 21.2 us -> 0 us
  starting transfers between devices: 0.54 us -> 21.3 us
    psum x4 -> x2, waiting for transfers between devices: 789 us -> 309 us  [the longest x1 276 us: per_device(): tail = lax.psum(tail, 'dp')]
    dot_general x100 -> x11, matrix products: 477 us -> 24.1 us  [the longest x2 9.41 us: per_device(): lax.dot_general(normed_two, dgu[i], along_rows, preferred_element_type=F32)]
    pallas_call x0 -> x16, Pallas kernels: none -> 186 us  [the longest x3 53 us: back_call(): pl.pallas_call(functools.partial(back_kernel, block, nb, shift), grid=(1,...]
    reduce_scatter x2 -> x0, waiting for transfers between devices: 99.6 us -> none  [the longest x1 54.8 us: per_device(): lax.psum_scatter(d_mixed_part, 'head', scatter_dimension=1, tiled=True)]
    dynamic_update_slice x42 -> x0, local copies, waits for them, and re-layouts: 90.7 us -> none  [the longest x12 69.8 us: per_device(): attended_blocks, log_totals = lax.map(forward_block, (query_blocks, starts))]
    all_gather x3 -> x2, waiting for transfers between devices: 84 us -> 0.01 us  [the longest x1 0.01 us: per_device(): cot = lax.all_gather(out_grad, 'head', axis=0, tiled=False)]
    ppermute x0 -> x41, waiting for transfers between devices: none -> 77.5 us  [per_device(): lax.ppermute(a, 'head', [(i, i ^ bit) for i in range(count)])]
    reduce_sum x24 -> x2, other arithmetic: 68.9 us -> 0.78 us  [the longest x1 0.69 us: per_device(): scale = lax.rsqrt(jnp.mean(x * x, -1, keepdims=True) + NORM_EPS)]
  transfers between devices with their start and end apart: 9 -> 45, of which waited for: 9 -> 18; matrix products, arithmetic and copies ran while one was open for 4% -> 10% of each run, Pallas kernels for 0% -> 21%
where the time goes in v1:
time: 734 us; the launch traced here: 725 us
  waiting for transfers between devices  388 us (53%)
  Pallas kernels  186 us (25%)
  local copies, waits for them, and re-layouts  48.2 us (7%)
  other arithmetic  41.7 us (6%)
  matrix products  24.1 us (3%)
  starting transfers between devices  21.3 us (3%)
  between operations  15.9 us (2%)
    psum x1, waiting for transfers between devices, per_device(): tail = lax.psum(tail, 'dp')  276 us
    ppermute x41, waiting for transfers between devices, per_device(): lax.ppermute(a, 'head', [(i, i ^ bit) for i in range(count)])  77.5 us
    pallas_call x3, Pallas kernels, back_call(): pl.pallas_call(functools.partial(back_kernel, block, nb, shift), grid=(1,...  53 us
    pallas_call x3, Pallas kernels, ffn_call(): pl.pallas_call(ffn_kernel, grid=(steps,), in_specs=[pl.BlockSpec(memory_s...  45.4 us
    psum x1, waiting for transfers between devices, per_device(): small = lax.psum(small, 'dp')  33.7 us
    pallas_call x3, Pallas kernels, unprep_call(): pl.pallas_call(functools.partial(unprep_kernel, block, nb, shift), grid=(...  28.9 us
    pallas_call x3, Pallas kernels, mix_call(): pl.pallas_call(functools.partial(mix_kernel, block, nb, shift, first, las...  27.9 us
    ppermute x41, starting transfers between devices, per_device(): lax.ppermute(a, 'head', [(i, i ^ bit) for i in range(count)])  21.2 us
  transfers between devices with their start and end apart: 45, of which 18 were waited for; matrix products, arithmetic and copies ran while one was open for 10% of the time, Pallas kernels for 21%

profile of v1, /device:TPU:0, one launch (start us, length us, event | category | flops | bytes accessed | tf_op | source)
XLA Modules:
  0.0 725.3 jit_solution(16969603611338404706)
XLA Ops:
  12.6 15.6 %prep.1 = (bf16[1536,256]{1,0:T(8,128)(2,1)}, bf16[1536,256]{1,0:T(8,128)(2,1)}, bf16[1536,256]{1,0:T(8,128)(2,1)}, bf16[256,1536]{1,0:T(8,128)(2,1)}, f32[3,153...) custom-call(s32[1]{0:T(128)S(6)} %copy.59.seq_ref.refs_0_, ...), custom_call_target="tpu_custom_call" | custom-call | tf_op jit(solution)/shard_map/prep/pallas_call | solution.py:138
  28.3 8.7 %mix_0.1 = (bf16[512,256]{1,0:T(8,128)(2,1)}, f32[512,256]{1,0:T(8,128)}, f32[512,256]{1,0:T(8,128)}, f32[512,256]{1,0:T(8,128)}, f32[256,256]{1,0:T(8,128)}, /*...) custom-call(s32[1]{0:T(128)S(6)} %copy.59.seq_ref.refs_0_, ...), custom_call_target="tpu_custom_call" | custom-call | tf_op jit(solution)/shard_map/mix_0/pallas_call | solution.py:298
  37.0 10.3 %mix_1.1 = (bf16[512,256]{1,0:T(8,128)(2,1)}, f32[512,256]{1,0:T(8,128)}, f32[512,256]{1,0:T(8,128)}, f32[512,256]{1,0:T(8,128)}, f32[256,256]{1,0:T(8,128)}, /*...) custom-call(s32[1]{0:T(128)S(6)} %copy.59.seq_ref.refs_0_, ...), custom_call_target="tpu_custom_call" | custom-call | tf_op jit(solution)/shard_map/mix_1/pallas_call | solution.py:298
  47.4 8.8 %mix_2.1 = (bf16[512,256]{1,0:T(8,128)(2,1)}, f32[512,256]{1,0:T(8,128)}, f32[512,256]{1,0:T(8,128)}, f32[512,256]{1,0:T(8,128)}) custom-call(s32[1]{0:T(128)S(6)} %copy.59.seq_ref.refs_0_, f32[24,128]{1,0:T(8,128)} %get-tuple-element.128.refs_1_.refs_14_, bf16[1536,256]{1,0:T(8,128)(2,1)} %get-tuple-element.129.refs_2_.refs_1_, ...), custom_call_target="tpu_custom_call" | custom-call | tf_op jit(solution)/shard_map/mix_2/pallas_call | solution.py:298
  61.2 8.1 %collective-permute-done.19.m2_ref = bf16[512,256]{1,0:T(8,128)(2,1)S(1)} collective-permute-done((bf16[512,256]{1,0:T(8,128)(2,1)}, bf16[512,256]{1,0:T(8,128)(2,1)S(1)}, u32[]{:S(2)}, u32[]{:S(2)}) %collective-permute-start.19) | collective-permute-done | bytes 262176 | tf_op jit(solution)/shard_map/ppermute | solution.py:894
  69.9 5.1 collective-permute-done.10.m2_ref
  83.9 15.1 %ffn_2.1 = (f32[512,1024]{1,0:T(8,128)}, bf16[512,1024]{1,0:T(8,128)(2,1)}, bf16[512,1024]{1,0:T(8,128)(2,1)}, bf16[2,512,1024]{2,1,0:T(8,128)(2,1)}, bf16[2,512...) custom-call(s32[4]{0:T(128)} %pad_add_fusion.peer_ref.refs_1_, ...), custom_call_target="tpu_custom_call" | custom-call | tf_op jit(solution)/shard_map/ffn_2/pallas_call | solution.py:390
  101.0 14.9 %ffn_1.1 = (f32[512,1024]{1,0:T(8,128)}, bf16[512,1024]{1,0:T(8,128)(2,1)}, bf16[512,1024]{1,0:T(8,128)(2,1)}, bf16[2,512,1024]{2,1,0:T(8,128)(2,1)}, bf16[2,512...) custom-call(s32[4]{0:T(128)} %pad_add_fusion.peer_ref.refs_1_, ...), custom_call_target="tpu_custom_call" | custom-call | tf_op jit(solution)/shard_map/ffn_1/pallas_call | solution.py:390
  117.4 15.4 %ffn_0.1 = (f32[512,1024]{1,0:T(8,128)}, bf16[512,1024]{1,0:T(8,128)(2,1)}, bf16[512,1024]{1,0:T(8,128)(2,1)}, bf16[2,512,1024]{2,1,0:T(8,128)(2,1)}, bf16[2,512...) custom-call(s32[4]{0:T(128)} %pad_add_fusion.peer_ref.refs_1_, ...), custom_call_target="tpu_custom_call" | custom-call | tf_op jit(solution)/shard_map/ffn_0/pallas_call | solution.py:390
  157.6 5.2 convert_bitcast_fusion
  167.7 10.7 %collective-permute-done.13.r2_ref = bf16[512,512]{1,0:T(8,128)(2,1)S(1)} collective-permute-done((bf16[512,512]{1,0:T(8,128)(2,1)S(1)}, bf16[512,512]{1,0:T(8,128)(2,1)S(1)}, u32[]{:S(2)}, u32[]{:S(2)}) %collective-permute-start.13) | collective-permute-done | bytes 524320 | tf_op jit(solution)/shard_map/ppermute | solution.py:894
  178.4 10.3 %collective-permute-done.4.r2_ref = bf16[512,512]{1,0:T(8,128)(2,1)S(1)} collective-permute-done((bf16[512,512]{1,0:T(8,128)(2,1)S(1)}, bf16[512,512]{1,0:T(8,128)(2,1)S(1)}, u32[]{:S(2)}, u32[]{:S(2)}) %collective-permute-start.4) | collective-permute-done | bytes 524320 | tf_op jit(solution)/shard_map/ppermute | solution.py:894
  198.7 16.6 %back_2.1 = (f32[512,256]{1,0:T(8,128)}, f32[1536,256]{1,0:T(8,128)}, f32[1536,256]{1,0:T(8,128)}, f32[2,16,256]{2,1,0:T(8,128)}, f32[256,256]{1,0:T(8,128)}, /*index=5*/f32[256,256]{1,0:T(8,128)}) custom-call(s32[1]{0:T(128)S(6)} %copy.59.seq_ref.refs_0_, bf16[1536,256]{1,0:T(8,128)(2,1)} %get-tuple-element.129.refs_2_.refs_1_, ...), custom_call_target="tpu_custom_call" | custom-call | tf_op jit(solution)/shard_map/back_2/pallas_call | solution.py:733
  215.2 9.0 %unprep_2.1 = (bf16[4,512,256]{2,1,0:T(8,128)(2,1)}, bf16[2,512,256]{2,1,0:T(8,128)(2,1)}, bf16[2,512,256]{2,1,0:T(8,128)(2,1)}, f32[8,512]{1,0:T(8,128)}, f32[1...) custom-call(s32[1]{0:T(128)S(6)} %copy.59.seq_ref.refs_0_, s32[4]{0:T(128)} %pad_add_fusion.peer_ref.refs_1_, ...), custom_call_target="tpu_custom_call" | custom-call | tf_op jit(solution)/shard_map/unprep_2/pallas_call | solution.py:852
  224.2 5.1 turn_1.1
  229.3 19.8 %back_1.1 = (f32[512,256]{1,0:T(8,128)}, f32[1024,256]{1,0:T(8,128)}, f32[1024,256]{1,0:T(8,128)}, f32[2,16,256]{2,1,0:T(8,128)}, f32[256,256]{1,0:T(8,128)}, /*...) custom-call(s32[1]{0:T(128)S(6)} %copy.59.seq_ref.refs_0_, ...), custom_call_target="tpu_custom_call" | custom-call | tf_op jit(solution)/shard_map/back_1/pallas_call | solution.py:733
  249.2 10.0 %unprep_1.1 = (bf16[4,512,256]{2,1,0:T(8,128)(2,1)}, bf16[2,512,256]{2,1,0:T(8,128)(2,1)}, bf16[2,512,256]{2,1,0:T(8,128)(2,1)}, f32[8,512]{1,0:T(8,128)}, f32[1...) custom-call(s32[1]{0:T(128)S(6)} %copy.59.seq_ref.refs_0_, s32[4]{0:T(128)} %pad_add_fusion.peer_ref.refs_1_, ...), custom_call_target="tpu_custom_call" | custom-call | tf_op jit(solution)/shard_map/unprep_1/pallas_call | solution.py:852
  265.1 16.6 %back_0.1 = (f32[512,256]{1,0:T(8,128)}, f32[512,256]{1,0:T(8,128)}, f32[512,256]{1,0:T(8,128)}, f32[2,16,256]{2,1,0:T(8,128)}, f32[256,256]{1,0:T(8,128)}, /*index=5*/f32[256,256]{1,0:T(8,128)}, f32[8,128]{1,0:T(8,128)}) custom-call(s32[1]{0:T(128)S(6)} %copy.59.seq_ref.refs_0_, bf16[1536,256]{1,0:T(8,128)(2,1)} %get-tuple-element.129.refs_2_.refs_1_, ...), custom_call_target="tpu_custom_call" | custom-call | tf_op jit(solution)/shard_map/back_0/pallas_call | solution.py:733
  281.7 10.0 %unprep_0.1 = (bf16[4,512,256]{2,1,0:T(8,128)(2,1)}, bf16[2,512,256]{2,1,0:T(8,128)(2,1)}, bf16[2,512,256]{2,1,0:T(8,128)(2,1)}, f32[8,512]{1,0:T(8,128)}, f32[1...) custom-call(s32[1]{0:T(128)S(6)} %copy.59.seq_ref.refs_0_, s32[4]{0:T(128)} %pad_add_fusion.peer_ref.refs_1_, ...), custom_call_target="tpu_custom_call" | custom-call | tf_op jit(solution)/shard_map/unprep_0/pallas_call | solution.py:852
  349.5 5.5 collective-permute-done.17
  367.5 33.7 %all-reduce.5.cloned.1.call-done = f32[100,256]{1,0:T(8,128)} async-done(((f32[100,256]{1,0:T(8,128)}), f32[100,256]{1,0:T(8,128)}) %all-reduce.5.cloned.1.call-update) | async-done | bytes 102416 | tf_op jit(solution)/shard_map/psum | solution.py:1017
  411.0 10.6 %collective-permute-done.32 = bf16[512,256]{1,0:T(8,128)(2,1)S(1)} collective-permute-done((bf16[512,256]{1,0:T(8,128)(2,1)S(1)}, bf16[512,256]{1,0:T(8,128)(2,1)S(1)}, u32[]{:S(2)}, u32[]{:S(2)}) %collective-permute-start.32) | collective-permute-done | bytes 262176 | tf_op jit(solution)/shard_map/ppermute | solution.py:894
  427.3 275.5 %all-reduce.7.cloned.1.call-done = (bf16[4,1024,256]{2,1,0:T(8,128)(2,1)}, bf16[4,64,256]{2,1,0:T(8,128)(2,1)}, bf16[4,256,64]{1,2,0:T(8,128)(2,1)}, bf16[1024,256]{1,0:T(8,128)(2,1)}, bf16[3,1024,1024]{2,1,0:T(8,128)(2,1)}) async-done(((bf16[4,1024,256]{2,1,0:T(8,128)(2,1)}, bf16[4,64,256]{2,1,0:T(8,128)(2,1)}, bf16[4,256,64]{1,2,0:T(8,128)(2,1)}, bf16[1024,256]{1,0:T(8,128)(2,1)}, ...) | async-done | bytes 9175056 | tf_op jit(solution)/shard_map/psum | solution.py:1016
  702.8 6.6 slice_convert_fusion
  (384 shorter events, 162.1 us)
Async XLA Ops:
  7.2 76.0 %all-gather.5.cloned.1.call-start = ((), (), s32[]{:S(2)}) async-start(), calls=%async_computation.1 | async-start | bytes 2621440 | tf_op jit(solution)/shard_map/all_gather | solution.py:895
  7.9 75.3 %all-gather.7.cloned.1.call-start = ((), (), s32[]{:S(2)}) async-start(), calls=%async_computation.2 | async-start | bytes 3932160 | tf_op jit(solution)/shard_map/all_gather | solution.py:896
  8.7 392.6 %all-reduce.5.cloned.1.call-start = ((), (), s32[]{:S(2)}) async-start(), calls=%async_computation | async-start | bytes 212992 | tf_op jit(solution)/shard_map/psum | solution.py:1017
  59.2 21.1 %collective-permute-start.1 = (bf16[512,256]{1,0:T(8,128)(2,1)S(1)}, bf16[512,256]{1,0:T(8,128)(2,1)S(1)}, u32[]{:S(2)}, u32[]{:S(2)}) collective-permute-start(bf16[512,256]{1,0:T(8,128)(2,1)S(1)} %copy-done.38), channel_id=1, source_target_pairs={{0,2},{1,3},{2,0},{3,1},{4,6},{5,7},{6,4},{7,5},{8,10},{9,11},{10,... | collective-permute-start | bytes 786440 | tf_op jit(solution)/shard_map/ppermute | solution.py:894
  69.3 30.3 %collective-permute-start.9 = (bf16[512,256]{1,0:T(8,128)(2,1)S(1)}, bf16[512,256]{1,0:T(8,128)(2,1)S(1)}, u32[]{:S(2)}, u32[]{:S(2)}) collective-permute-start(bf16[512,256]{1,0:T(8,128)(2,1)S(1)} %copy-done.44), channel_id=1, source_target_pairs={{0,1},{1,0},{2,3},{3,2},{4,5},{5,4},{6,7},{7,6},{8,9},{9,8},{10,11... | collective-permute-start | bytes 786440 | tf_op jit(solution)/shard_map/ppermute | solution.py:894
  75.0 24.7 %collective-permute-start.11 = (bf16[512,256]{1,0:T(8,128)(2,1)S(1)}, bf16[512,256]{1,0:T(8,128)(2,1)S(1)}, u32[]{:S(2)}, u32[]{:S(2)}) collective-permute-start(bf16[512,256]{1,0:T(8,128)(2,1)S(1)} %collective-permute-done.10.m2_ref), channel_id=1, source_target_pairs={{0,1},{1,0},{2,3},{3,2},{4,5},{5,4},{6,7},{7,6},{8,9},{9,8},{10,11... | collective-permute-start | bytes 786440 | tf_op jit(solution)/shard_map/ppermute | solution.py:894
  75.0 41.0 %collective-permute-start = (bf16[512,256]{1,0:T(8,128)(2,1)S(1)}, bf16[512,256]{1,0:T(8,128)(2,1)S(1)}, u32[]{:S(2)}, u32[]{:S(2)}) collective-permute-start(bf16[512,256]{1,0:T(8,128)(2,1)S(1)} %copy-done.38), channel_id=1, source_target_pairs={{0,1},{1,0},{2,3},{3,2},{4,5},{5,4},{6,7},{7,6},{8,9},{9,8},{10,11... | collective-permute-start | bytes 786440 | tf_op jit(solution)/shard_map/ppermute | solution.py:894
  80.3 35.7 %collective-permute-start.2 = (bf16[512,256]{1,0:T(8,128)(2,1)S(1)}, bf16[512,256]{1,0:T(8,128)(2,1)S(1)}, u32[]{:S(2)}, u32[]{:S(2)}) collective-permute-start(bf16[512,256]{1,0:T(8,128)(2,1)S(1)} %collective-permute-done.1.m2_ref), channel_id=1, source_target_pairs={{0,1},{1,0},{2,3},{3,2},{4,5},{5,4},{6,7},{7,6},{8,9},{9,8},{10,11... | collective-permute-start | bytes 786440 | tf_op jit(solution)/shard_map/ppermute | solution.py:894
  99.0 51.8 %collective-permute-start.21 = (bf16[512,512]{1,0:T(8,128)(2,1)}, bf16[512,512]{1,0:T(8,128)(2,1)}, u32[]{:S(2)}, u32[]{:S(2)}) collective-permute-start(bf16[512,512]{1,0:T(8,128)(2,1)} %get-tuple-element.159), channel_id=1, source_target_pairs={{0,1},{1,0},{2,3},{3,2},{4,5},{5,4},{6,7},{7,6},{8,9},{9,8},{10,11... | collective-permute-start | bytes 1572872 | tf_op jit(solution)/shard_map/ppermute | solution.py:894
  115.9 36.8 %collective-permute-start.12 = (bf16[512,512]{1,0:T(8,128)(2,1)}, bf16[512,512]{1,0:T(8,128)(2,1)}, u32[]{:S(2)}, u32[]{:S(2)}) collective-permute-start(bf16[512,512]{1,0:T(8,128)(2,1)} %get-tuple-element.149), channel_id=1, source_target_pairs={{0,1},{1,0},{2,3},{3,2},{4,5},{5,4},{6,7},{7,6},{8,9},{9,8},{10,11... | collective-permute-start | bytes 1572872 | tf_op jit(solution)/shard_map/ppermute | solution.py:894
  154.1 24.3 %collective-permute-start.13 = (bf16[512,512]{1,0:T(8,128)(2,1)S(1)}, bf16[512,512]{1,0:T(8,128)(2,1)S(1)}, u32[]{:S(2)}, u32[]{:S(2)}) collective-permute-start(bf16[512,512]{1,0:T(8,128)(2,1)S(1)} %add_convert_fusion.6.s1_ref), channel_id=1, source_target_pairs={{0,2},{1,3},{2,0},{3,1},{4,6},{5,7},{6,4},{7,5},{8,10},{9,11},{10,... | collective-permute-start | bytes 1572872 | tf_op jit(solution)/shard_map/ppermute | solution.py:894
  157.2 31.5 %collective-permute-start.4 = (bf16[512,512]{1,0:T(8,128)(2,1)S(1)}, bf16[512,512]{1,0:T(8,128)(2,1)S(1)}, u32[]{:S(2)}, u32[]{:S(2)}) collective-permute-start(bf16[512,512]{1,0:T(8,128)(2,1)S(1)} %add_convert_fusion.8.s1_ref), channel_id=1, source_target_pairs={{0,2},{1,3},{2,0},{3,1},{4,6},{5,7},{6,4},{7,5},{8,10},{9,11},{10,... | collective-permute-start | bytes 1572872 | tf_op jit(solution)/shard_map/ppermute | solution.py:894
  162.8 61.4 %collective-permute-start.14 = (bf16[512,512]{1,0:T(8,128)(2,1)S(1)}, bf16[512,512]{1,0:T(8,128)(2,1)}, u32[]{:S(2)}, u32[]{:S(2)}) collective-permute-start(bf16[512,512]{1,0:T(8,128)(2,1)S(1)} %add_convert_fusion.6.s1_ref), channel_id=1, source_target_pairs={{0,1},{1,0},{2,3},{3,2},{4,5},{5,4},{6,7},{7,6},{8,9},{9,8},{10,11... | collective-permute-start | bytes 1572872 | tf_op jit(solution)/shard_map/ppermute | solution.py:894
  167.2 91.9 %collective-permute-start.5 = (bf16[512,512]{1,0:T(8,128)(2,1)S(1)}, bf16[512,512]{1,0:T(8,128)(2,1)S(1)}, u32[]{:S(2)}, u32[]{:S(2)}) collective-permute-start(bf16[512,512]{1,0:T(8,128)(2,1)S(1)} %add_convert_fusion.8.s1_ref), channel_id=1, source_target_pairs={{0,1},{1,0},{2,3},{3,2},{4,5},{5,4},{6,7},{7,6},{8,9},{9,8},{10,11... | collective-permute-start | bytes 1572872 | tf_op jit(solution)/shard_map/ppermute | solution.py:894
  167.2 25.6 %collective-permute-start.24 = (bf16[512,512]{1,0:T(8,128)(2,1)S(1)}, bf16[512,512]{1,0:T(8,128)(2,1)S(1)}, u32[]{:S(2)}, u32[]{:S(2)}) collective-permute-start(bf16[512,512]{1,0:T(8,128)(2,1)S(1)} %collective-permute-done.22.r2_ref), channel_id=1, source_target_pairs={{0,1},{1,0},{2,3},{3,2},{4,5},{5,4},{6,7},{7,6},{8,9},{9,8},{10,11... | collective-permute-start | bytes 1572872 | tf_op jit(solution)/shard_map/ppermute | solution.py:894
  178.4 45.8 %collective-permute-start.15 = (bf16[512,512]{1,0:T(8,128)(2,1)S(1)}, bf16[512,512]{1,0:T(8,128)(2,1)}, u32[]{:S(2)}, u32[]{:S(2)}) collective-permute-start(bf16[512,512]{1,0:T(8,128)(2,1)S(1)} %collective-permute-done.13.r2_ref), channel_id=1, source_target_pairs={{0,1},{1,0},{2,3},{3,2},{4,5},{5,4},{6,7},{7,6},{8,9},{9,8},{10,11... | collective-permute-start | bytes 1572872 | tf_op jit(solution)/shard_map/ppermute | solution.py:894
  188.7 70.4 %collective-permute-start.6 = (bf16[512,512]{1,0:T(8,128)(2,1)S(1)}, bf16[512,512]{1,0:T(8,128)(2,1)S(1)}, u32[]{:S(2)}, u32[]{:S(2)}) collective-permute-start(bf16[512,512]{1,0:T(8,128)(2,1)S(1)} %collective-permute-done.4.r2_ref), channel_id=1, source_target_pairs={{0,1},{1,0},{2,3},{3,2},{4,5},{5,4},{6,7},{7,6},{8,9},{9,8},{10,11... | collective-permute-start | bytes 1572872 | tf_op jit(solution)/shard_map/ppermute | solution.py:894
  303.1 23.2 %collective-permute-start.39 = (f32[2,1024]{1,0:T(2,128)}, f32[2,1024]{1,0:T(2,128)}, u32[]{:S(2)}, u32[]{:S(2)}) collective-permute-start(f32[2,1024]{1,0:T(2,128)} %pad_maximum_fusion.6), channel_id=1, source_target_pairs={{0,1},{1,0},{2,3},{3,2},{4,5},{5,4},{6,7},{7,6},{8,9},{9,8},{10,11... | collective-permute-start | bytes 24584 | tf_op jit(solution)/shard_map/ppermute | solution.py:894
  332.2 370.6 %all-reduce.7.cloned.1.call-start = ((), (), s32[]{:S(2)}) async-start(), calls=%async_computation.3 | async-start | bytes 18350080 | tf_op jit(solution)/shard_map/psum | solution.py:1016
  342.7 17.1 %collective-permute-start.8 = (bf16[512,256]{1,0:T(8,128)(2,1)S(1)}, bf16[512,256]{1,0:T(8,128)(2,1)S(1)}, u32[]{:S(2)}, u32[]{:S(2)}) collective-permute-start(bf16[512,256]{1,0:T(8,128)(2,1)S(1)} %slice_bitcast_fusion.27), channel_id=1, source_target_pairs={{0,2},{1,3},{2,0},{3,1},{4,6},{5,7},{6,4},{7,5},{8,10},{9,11},{10,... | collective-permute-start | bytes 786440 | tf_op jit(solution)/shard_map/ppermute | solution.py:894
  343.9 63.0 %collective-permute-start.27 = (bf16[2,512,256]{2,1,0:T(8,128)(2,1)}, bf16[2,512,256]{2,1,0:T(8,128)(2,1)S(1)}, u32[]{:S(2)}, u32[]{:S(2)}) collective-permute-start(bf16[2,512,256]{2,1,0:T(8,128)(2,1)} %get-tuple-element.205), channel_id=1, source_target_pairs={{0,1},{1,0},{2,3},{3,2},{4,5},{5,4},{6,7},{7,6},{8,9},{9,8},{10,11... | collective-permute-start | bytes 1572872 | tf_op jit(solution)/shard_map/ppermute | solution.py:894
  343.9 16.0 %collective-permute-start.29 = (f32[8,512]{1,0:T(8,128)S(1)}, f32[8,512]{1,0:T(8,128)S(1)}, u32[]{:S(2)}, u32[]{:S(2)}) collective-permute-start(f32[8,512]{1,0:T(8,128)S(1)} %copy-done.78), channel_id=1, source_target_pairs={{0,1},{1,0},{2,3},{3,2},{4,5},{5,4},{6,7},{7,6},{8,9},{9,8},{10,11... | collective-permute-start | bytes 49160 | tf_op jit(solution)/shard_map/ppermute | solution.py:894
  355.0 54.3 %collective-permute-start.35 = (bf16[2,512,256]{2,1,0:T(8,128)(2,1)}, bf16[2,512,256]{2,1,0:T(8,128)(2,1)S(1)}, u32[]{:S(2)}, u32[]{:S(2)}) collective-permute-start(bf16[2,512,256]{2,1,0:T(8,128)(2,1)} %get-tuple-element.213), channel_id=1, source_target_pairs={{0,1},{1,0},{2,3},{3,2},{4,5},{5,4},{6,7},{7,6},{8,9},{9,8},{10,11... | collective-permute-start | bytes 1572872 | tf_op jit(solution)/shard_map/ppermute | solution.py:894
  361.3 47.3 %collective-permute-start.31 = (bf16[2,512,256]{2,1,0:T(8,128)(2,1)}, bf16[2,512,256]{2,1,0:T(8,128)(2,1)S(1)}, u32[]{:S(2)}, u32[]{:S(2)}) collective-permute-start(bf16[2,512,256]{2,1,0:T(8,128)(2,1)} %get-tuple-element.209), channel_id=1, source_target_pairs={{0,1},{1,0},{2,3},{3,2},{4,5},{5,4},{6,7},{7,6},{8,9},{9,8},{10,11... | collective-permute-start | bytes 1572872 | tf_op jit(solution)/shard_map/ppermute | solution.py:894
  (110 other events, 1218.6 us)
Sparse Core Ops, SparseCore 0:
  9.6 25.2 all-gather.4
  36.4 31.8 all-gather.6
  332.3 68.8 all-reduce.4
  408.1 294.6 all-reduce.6

commit v2 on v1

--- a/solution.py
+++ b/solution.py
@@ -16,6 +16,8 @@
 SPAN = 512
 HALO = 8
 GATE_ROWS = 128
+COST_UNIT = 1.5e8
+SMALL_ROWS = 1024
 
 
 def dot_nn(left, right):
@@ -35,6 +37,12 @@
 
 def iota(shape, axis):
     return lax.broadcasted_iota(jnp.int32, shape, axis)
+
+
+def cost(microseconds):
+    return pl.CostEstimate(
+        flops=int(microseconds * COST_UNIT), transcendentals=0, bytes_accessed=1 << 20
+    )
 
 
 def head_blocks(cols, shift):
@@ -172,6 +180,7 @@
             jax.ShapeDtypeStruct(pers.shape, BF16),
         ],
         scratch_shapes=[pltpu.VMEM((3, HALO + SPAN, cols), F32)],
+        cost_estimate=cost(15),
         name="prep",
     )(seq, x, w, conv, gains, gate, pers)
 
@@ -302,33 +311,23 @@
         out_specs=out_specs,
         out_shape=outs,
         scratch_shapes=scratch,
+        cost_estimate=cost(9),
         name=f"mix_{block}",
     )(*ins)
 
 
-def ffn_kernel(
-    peer_ref,
-    x_ref,
-    m0_ref,
-    m1_ref,
-    m2_ref,
-    m3_ref,
-    ow_ref,
-    gain_ref,
-    fin_ref,
-    fout_ref,
-    cot_ref,
-    res_ref,
-    nt_ref,
-    hid_ref,
-    dgu_ref,
-    part_keep_ref,
-    part_send_ref,
-    dn_keep_ref,
-    dn_send_ref,
-    gg_ref,
-    part_ref,
-):
+def ffn_kernel(first_call, *refs):
+    it = iter(refs)
+    take = lambda n: [next(it) for _ in range(n)]
+    peer_ref, x_ref, m0_ref, m1_ref, m2_ref, m3_ref = take(6)
+    ow_ref, gain_ref, fin_ref, fout_ref, cot_ref = take(5)
+    if not first_call:
+        gg_in_ref = take(8)[0]
+    gg_ref, nt_ref, hid_ref, dgu_ref, part_keep_ref, part_send_ref, cotf_ref, mfull_ref = take(8)
+    res_ref, dn_keep_ref, dn_send_ref = take(3)
+    if first_call:
+        take(1)
+    (part_ref,) = take(1)
     rows, width = x_ref.shape
     cols = m0_ref.shape[1]
     shards = width // cols
@@ -336,6 +335,7 @@
     for j, m_ref in enumerate((m0_ref, m1_ref, m2_ref, m3_ref)):
         at = pl.ds(pl.multiple_of(peer_ref[j] * cols, cols), cols)
         weight = jnp.concatenate([ow_ref[p, at, :] for p in range(shards)], 1)
+        mfull_ref[:, at] = m_ref[...]
         term = dot_nn(m_ref[...], weight)
         branch = term if branch is None else branch + term
     residual = x_ref[...].astype(F32) + branch
@@ -350,6 +350,7 @@
     hidden = (silu * up_pre).astype(BF16)
     hid_ref[...] = hidden
     cot = jnp.concatenate([cot_ref[p] for p in range(shards)], 1)
+    cotf_ref[...] = cot
     d_hidden = dot_nt(cot, fout_ref[...])
     slope = sig * (1.0 + gate_pre * (1.0 - sig))
     d_gate = (d_hidden * up_pre * slope).astype(BF16)
@@ -361,7 +362,7 @@
 
     @pl.when(pl.program_id(0) == 0)
     def _():
-        gg_ref[...] = jnp.zeros_like(gg_ref)
+        gg_ref[...] = jnp.zeros(gg_ref.shape, F32) if first_call else gg_in_ref[...]
 
     gg_ref[...] = gg_ref[...] + jnp.broadcast_to(gains, gg_ref.shape)
     half = width // 2
@@ -376,8 +377,8 @@
             out_ref[n] = part_ref[:, pl.ds(start, cols)]
 
 
-def ffn_call(block, peers, x, mixed, ow, gains, fin, fout, cot):
-    width = x.shape[1]
+def ffn_call(block, peers, x, mixed, ow, gains, fin, fout, cot, shared):
+    rows, width = x.shape
     cols = mixed[0].shape[1]
     tile = SPAN // 2
     steps = SPAN // tile
@@ -385,70 +386,78 @@
     hidden = fout.shape[0]
     whole = lambda a: pl.BlockSpec(a.shape, lambda i, n=a.ndim: (0,) * n)
     row = lambda n: pl.BlockSpec((tile, n), lambda i: (i, 0))
-    stacked = lambda n, w: pl.BlockSpec((n, tile, w), lambda i: (0, i, 0))
+    at_rows = lambda n: pl.BlockSpec((tile, n), lambda i: (block * steps + i, 0))
+    stacked = lambda n, w: pl.BlockSpec((n, tile, w), lambda i: (0, block * steps + i, 0))
     struct = jax.ShapeDtypeStruct
-    return pl.pallas_call(
-        ffn_kernel,
+    ins = [peers, x, *mixed, ow, gains, fin, fout, cot]
+    in_specs = [
+        pl.BlockSpec(memory_space=pltpu.SMEM),
+        at_rows(width),
+        row(cols),
+        row(cols),
+        row(cols),
+        row(cols),
+        whole(ow),
+        whole(gains),
+        whole(fin),
+        whole(fout),
+        stacked(shards, cols),
+    ]
+    aliases = {}
+    if shared is not None:
+        aliases = {len(ins) + n: n for n in range(len(shared))}
+        ins += shared
+        in_specs += [pl.BlockSpec((8, width), lambda i: (0, 0))]
+        in_specs += [pl.BlockSpec(memory_space=pl.ANY)] * (len(shared) - 1)
+    room = [struct((3 * width, width), BF16)] if shared is None else []
+    got = pl.pallas_call(
+        functools.partial(ffn_kernel, shared is None),
         grid=(steps,),
-        in_specs=[
-            pl.BlockSpec(memory_space=pltpu.SMEM),
-            pl.BlockSpec((tile, width), lambda i: (block * steps + i, 0)),
-            row(cols),
-            row(cols),
-            row(cols),
-            row(cols),
-            whole(ow),
-            whole(gains),
-            whole(fin),
-            whole(fout),
-            pl.BlockSpec((shards, tile, cols), lambda i: (0, block * steps + i, 0)),
-        ],
+        in_specs=in_specs,
         out_specs=[
-            row(width),
-            row(width),
-            row(hidden),
+            pl.BlockSpec((8, width), lambda i: (0, 0)),
+            at_rows(width),
+            at_rows(hidden),
             stacked(2, hidden),
             stacked(2, cols),
             stacked(2, cols),
+            at_rows(width),
+            at_rows(width),
+            row(width),
             row(width // 2),
             row(width // 2),
-            pl.BlockSpec((8, width), lambda i: (0, 0)),
-        ],
+        ]
+        + [pl.BlockSpec(memory_space=pl.ANY)] * len(room),
         out_shape=[
+            struct((8, width), F32),
+            struct((rows, width), BF16),
+            struct((rows, hidden), BF16),
+            struct((2, rows, hidden), BF16),
+            struct((2, rows, cols), BF16),
+            struct((2, rows, cols), BF16),
+            struct((rows, width), BF16),
+            struct((rows, width), BF16),
             struct((SPAN, width), F32),
-            struct((SPAN, width), BF16),
-            struct((SPAN, hidden), BF16),
-            struct((2, SPAN, hidden), BF16),
-            struct((2, SPAN, cols), BF16),
-            struct((2, SPAN, cols), BF16),
             struct((SPAN, width // 2), BF16),
             struct((SPAN, width // 2), BF16),
-            struct((8, width), F32),
-        ],
+        ]
+        + room,
+        input_output_aliases=aliases,
         scratch_shapes=[pltpu.VMEM((tile, width), BF16)],
+        cost_estimate=cost(15),
         name=f"ffn_{block}",
-    )(peers, x, *mixed, ow, gains, fin, fout, cot)
-
-
-def turn_kernel(
-    peer_ref,
-    s1_ref,
-    r2_ref,
-    ps1_ref,
-    pr2_ref,
-    res_ref,
-    cot_ref,
-    ow_ref,
-    gain_ref,
-    gp_ref,
-    tot_ref,
-    dres_ref,
-    rescol_ref,
-    dbr_ref,
-    dga_ref,
-    dgp_ref,
-    full_ref,
-):
+    )(*ins)
+    return got[:8], got[8:]
+
+
+def turn_kernel(first_call, *refs):
+    it = iter(refs)
+    take = lambda n: [next(it) for _ in range(n)]
+    peer_ref, s1_ref, r2_ref, ps1_ref, pr2_ref, res_ref, cot_ref, ow_ref = take(8)
+    gain_ref, gp_ref, tot_ref = take(3)
+    if not first_call:
+        take(4)
+    dres_ref, rescol_ref, dbr_ref, dgall_ref, dga_ref, dgp_ref, full_ref = take(7)
     rows, width = res_ref.shape
     cols = gp_ref.shape[1]
     shards = width // cols
@@ -476,45 +485,59 @@
     gate = jax.nn.sigmoid(gp_ref[...])
     d_gated = d_mixed * gate
     dga_ref[...] = d_gated.astype(BF16)
-    dgp_ref[...] = (d_gated * tot_ref[...] * (1.0 - gate)).astype(BF16)
-
-
-def turn_call(block, peers, pieces, res, cot, ow, gains, gp, tot):
+    d_gate = (d_gated * tot_ref[...] * (1.0 - gate)).astype(BF16)
+    dgp_ref[...] = d_gate
+    dgall_ref[...] = d_gate
+
+
+def turn_call(block, peers, pieces, res, cot, ow, gains, gp, tot, shared):
     width = res.shape[1]
-    cols = gp.shape[1]
+    rows, cols = gp.shape
     tile = SPAN // 2
     steps = SPAN // tile
     shards = width // cols
     whole = lambda a: pl.BlockSpec(a.shape, lambda i, n=a.ndim: (0,) * n)
     row = lambda n: pl.BlockSpec((tile, n), lambda i: (i, 0))
+    at_rows = lambda n: pl.BlockSpec((tile, n), lambda i: (block * steps + i, 0))
     struct = jax.ShapeDtypeStruct
-    return pl.pallas_call(
-        turn_kernel,
+    ins = [peers, *pieces, res, cot, ow, gains, gp, tot]
+    in_specs = [
+        pl.BlockSpec(memory_space=pltpu.SMEM),
+        row(width // 2),
+        row(width // 2),
+        row(width // 2),
+        row(width // 2),
+        row(width),
+        pl.BlockSpec((shards, tile, cols), lambda i: (0, block * steps + i, 0)),
+        whole(ow),
+        whole(gains),
+        at_rows(cols),
+        row(cols),
+    ]
+    aliases = {}
+    if shared is not None:
+        aliases = {len(ins) + n: n for n in range(len(shared))}
+        ins += shared
+        in_specs += [pl.BlockSpec(memory_space=pl.ANY)] * len(shared)
+    got = pl.pallas_call(
+        functools.partial(turn_kernel, shared is None),
         grid=(steps,),
-        in_specs=[
-            pl.BlockSpec(memory_space=pltpu.SMEM),
-            row(width // 2),
-            row(width // 2),
-            row(width // 2),
-            row(width // 2),
-            row(width),
-            pl.BlockSpec((shards, tile, cols), lambda i: (0, block * steps + i, 0)),
-            whole(ow),
-            whole(gains),
-            pl.BlockSpec((tile, cols), lambda i: (block * steps + i, 0)),
-            row(cols),
-        ],
-        out_specs=[row(cols)] * 5,
+        in_specs=in_specs,
+        out_specs=[at_rows(cols)] * 4 + [row(cols)] * 2,
         out_shape=[
-            struct((SPAN, cols), F32),
-            struct((SPAN, cols), F32),
-            struct((SPAN, cols), BF16),
+            struct((rows, cols), F32),
+            struct((rows, cols), F32),
+            struct((rows, cols), BF16),
+            struct((rows, cols), BF16),
             struct((SPAN, cols), BF16),
             struct((SPAN, cols), BF16),
         ],
+        input_output_aliases=aliases,
         scratch_shapes=[pltpu.VMEM((tile, width), F32)],
+        cost_estimate=cost(5),
         name=f"turn_{block}",
-    )(peers, *pieces, res, cot, ow, gains, gp, tot)
+    )(*ins)
+    return got[:4], got[4:]
 
 
 def back_kernel(block, nb, shift, *refs):
@@ -737,6 +760,7 @@
         out_specs=[whole(s) for s in shapes],
         out_shape=[jax.ShapeDtypeStruct(s, F32) for s in shapes],
         scratch_shapes=scratch,
+        cost_estimate=cost(17),
         name=f"back_{block}",
     )(*ins)
     return dict(zip(names, outs))
@@ -748,9 +772,14 @@
     first, last = block == 0, block == nb - 1
     seq_ref, peer_ref, dq_ref, dk_ref, dv_ref, dgp_ref, pre_ref, w_ref, conv_ref = take(9)
     x_ref, gain_ref = take(2)
-    (halo_ref,) = (None,) if first else take(1)
-    next_ref, dlg_ref, gate_ref = (None, None, None) if last else take(3)
-    dproj_ref, keep_ref, send_ref, inner_ref, cg_ref, gg_ref, edge_ref = take(7)
+    halo_ref = None if first else take(1)[0]
+    dp_ref, pers_ref, ab_ref, btb_ref, gain_two_ref = take(5) if first else [None] * 5
+    if not last:
+        edge_in_ref, dlg_ref, gate_ref, mean_ref = take(4)
+        cg_in_ref, gg_in_ref, gate_in_ref = take(7)[:3]
+    cg_ref, gg_ref, gate_out_ref = take(3)
+    dproj_ref, keep_ref, send_ref, inner_ref, edge_ref = take(5)
+    small_ref, gains_ref = take(2) if first else (None, None)
     ext_ref, dext_ref, low_ref = take(3)
     rows, cols = dq_ref.shape
     width = x_ref.shape[1]
@@ -758,7 +787,13 @@
     taps = conv_ref.shape[1]
     d_normed = dot_nt(dgp_ref[...], w_ref[3])
     dproj_ref[3] = dgp_ref[...]
-    cg_ref[...] = jnp.zeros(cg_ref.shape, F32)
+    if last:
+        cg_ref[...] = jnp.zeros(cg_ref.shape, F32)
+        gg_ref[...] = jnp.zeros(gg_ref.shape, F32)
+        gate_out_ref[...] = jnp.zeros(gate_out_ref.shape, F32)
+    else:
+        cg_ref[...] = cg_in_ref[...]
+        gg_ref[...] = gg_in_ref[...]
     for i in range(3):
         pre = pre_ref[i]
         ext_ref[0:HALO, :] = jnp.zeros((HALO, cols), F32) if first else halo_ref[i]
@@ -777,15 +812,14 @@
         edge_ref[i] = d_conv[0:HALO, :]
         dext_ref[0:rows, :] = d_conv
         dext_ref[rows : rows + HALO, :] = (
-            jnp.zeros((HALO, cols), F32) if last else next_ref[i]
+            jnp.zeros((HALO, cols), F32) if last else edge_in_ref[i]
         )
         d_pre = conv_ref[i, 0:1, :] * d_conv
         for j in range(taps):
             if j:
                 d_pre = d_pre + conv_ref[i, j : j + 1, :] * dext_ref[j : j + rows, :]
-            cg_ref[i * taps + j : i * taps + j + 1, :] = jnp.sum(
-                d_conv * shifted[j], 0, keepdims=True
-            )
+            at = slice(i * taps + j, i * taps + j + 1)
+            cg_ref[at, :] = cg_ref[at, :] + jnp.sum(d_conv * shifted[j], 0, keepdims=True)
         d_low = d_pre.astype(BF16)
         dproj_ref[i] = d_low
         d_normed = d_normed + dot_nt(d_low, w_ref[i])
@@ -795,10 +829,19 @@
             dlg_ref[...], gate_ref[...], preferred_element_type=F32, precision=HIGH
         )
         d_normed = d_normed + (valid / count) * d_mean[0:1, :]
+        outer = lax.dot_general(
+            dlg_ref[...] * 0.125,
+            mean_ref[...],
+            (((0,), (0,)), ((), ())),
+            preferred_element_type=F32,
+            precision=HIGH,
+        )
+        gate_out_ref[...] = gate_in_ref[...] + outer[0 : gate_out_ref.shape[0], :]
     x = x_ref[...].astype(F32)
     scale = lax.rsqrt(jnp.mean(x * x, -1, keepdims=True) + NORM_EPS)
     weighted = d_normed * x
-    gg_ref[...] = jnp.broadcast_to(jnp.sum(weighted * scale, 0, keepdims=True), gg_ref.shape)
+    gains = jnp.sum(weighted * scale, 0, keepdims=True)
+    gg_ref[...] = gg_ref[...] + jnp.broadcast_to(gains, gg_ref.shape)
     ones = jnp.ones((8, width), BF16)
     high, rest = two_parts(weighted * gain_ref[0:1, :])
     inner_ref[...] = dot_nt(ones, high) + dot_nt(ones, rest)
@@ -807,15 +850,56 @@
         for n in range(2):
             start = pl.multiple_of(peer_ref[slot + 2 * n] * cols, cols)
             out_ref[n] = low_ref[:, pl.ds(start, cols)]
-
-
-def unprep_call(block, nb, shift, seq, peers, back, dgp, pre, w, conv, x, gains, edge, gate):
+    if first:
+        keys = pers_ref[0]
+        d_keys = dp_ref[0]
+        scale = lax.rsqrt(head_sum(keys * keys, blocks) + UNIT_EPS)
+        along = head_sum(d_keys * keys, blocks)
+        d_keys = scale * (d_keys - keys * (scale * scale * along))
+        across = lambda a: [a[:, n : n + cols] for n in range(0, width, cols)]
+        parts = [ab_ref[...], btb_ref[...], *across(gate_out_ref[...]), cg_ref[...]]
+        parts += [d_keys, dp_ref[1]]
+        at = 0
+        for part in parts:
+            small_ref[at : at + part.shape[0], :] = part.astype(BF16)
+            at += part.shape[0]
+        gains_ref[0:1, :] = gg_ref[0:1, :]
+        gains_ref[1:2, :] = gain_two_ref[0:1, :]
+        small_ref[at:, :] = jnp.zeros((small_ref.shape[0] - at, cols), BF16)
+
+
+def unprep_call(
+    block, nb, shift, seq, peers, back, dgp, pre, w, conv, x, gains, gate, mean, pers, gain_two,
+    shared,
+):
+    rows, width = x.shape
     cols = dgp.shape[1]
-    width = x.shape[1]
     first, last = block == 0, block == nb - 1
-    whole = lambda a: pl.BlockSpec(a.shape, lambda i, n=a.ndim: (0,) * n)
+    whole = lambda a: pl.BlockSpec(a.shape, lambda i, n=len(a.shape): (0,) * n)
     smem = pl.BlockSpec(memory_space=pltpu.SMEM)
     at_block = pl.BlockSpec((SPAN, cols), lambda i: (block, 0))
+    stacked = lambda n: pl.BlockSpec((n, SPAN, cols), lambda i: (0, block, 0))
+    struct = jax.ShapeDtypeStruct
+    gate_rows_out = 16
+    names = ["cg", "gg", "gate", "dproj", "keep", "send", "inner", "edge"]
+    outs = [
+        struct((16, cols), F32),
+        struct((8, width), F32),
+        struct((gate_rows_out, width), F32),
+        struct((4, rows, cols), BF16),
+        struct((2, rows, cols), BF16),
+        struct((2, rows, cols), BF16),
+        struct((8, rows), F32),
+        struct((3, HALO, cols), F32),
+    ]
+    out_specs = [whole(a) for a in outs[:3]]
+    out_specs += [
+        stacked(4),
+        stacked(2),
+        stacked(2),
+        pl.BlockSpec((8, SPAN), lambda i: (0, block)),
+        whole(outs[7]),
+    ]
     ins = [seq, peers, back["dq"], back["dk"], back["dv"], dgp, pre, w, conv, x, gains]
     in_specs = [
         smem,
@@ -824,48 +908,119 @@
         at_block,
         at_block,
         whole(dgp),
-        pl.BlockSpec((3, SPAN, cols), lambda i: (0, block, 0)),
+        stacked(3),
         whole(w),
         whole(conv),
         pl.BlockSpec((SPAN, width), lambda i: (block, 0)),
         whole(gains),
     ]
+    aliases = {}
     if not first:
         ins.append(pre)
         in_specs.append(
             pl.BlockSpec((3, HALO, cols), lambda i: (0, block * (SPAN // HALO) - 1, 0))
         )
-    if not last:
-        ins += [edge, back["dlg"], gate]
-        in_specs += [whole(edge), whole(back["dlg"]), whole(gate)]
-    struct = jax.ShapeDtypeStruct
-    outs = [
-        struct((4, SPAN, cols), BF16),
-        struct((2, SPAN, cols), BF16),
-        struct((2, SPAN, cols), BF16),
-        struct((8, SPAN), F32),
-        struct((16, cols), F32),
-        struct((8, width), F32),
-        struct((3, HALO, cols), F32),
-    ]
-    names = ["dproj", "keep", "send", "inner", "cg", "gg", "edge"]
+    else:
+        others = [back["dp"], pers, back["ab"], back["btb"], gain_two]
+        ins += others
+        in_specs += [whole(a) for a in others]
+        names += ["small", "gains"]
+        ahead = 5 * width // SMALL_ROWS
+        outs.append(struct(((ahead + 1) * SMALL_ROWS, cols), BF16))
+        out_specs.append(pl.BlockSpec((SMALL_ROWS, cols), lambda i: (ahead, 0)))
+        outs.append(struct((2, width), F32))
+        out_specs.append(whole(outs[-1]))
+    if not last:
+        ins += [shared["edge"], back["dlg"], gate, mean]
+        in_specs += [whole(shared["edge"]), whole(back["dlg"]), whole(gate)]
+        in_specs.append(pl.BlockSpec((8, width), lambda i: (block, 0)))
+        aliases = {len(ins) + n: n for n in range(7)}
+        ins += [shared[name] for name in names[:7]]
+        in_specs += [whole(a) for a in outs[:3]] + [pl.BlockSpec(memory_space=pl.ANY)] * 4
     got = pl.pallas_call(
         functools.partial(unprep_kernel, block, nb, shift),
         grid=(1,),
         in_specs=in_specs,
-        out_specs=[pl.BlockSpec(s.shape, lambda i, n=len(s.shape): (0,) * n) for s in outs],
+        out_specs=out_specs,
         out_shape=outs,
+        input_output_aliases=aliases,
         scratch_shapes=[
             pltpu.VMEM((HALO + SPAN, cols), F32),
             pltpu.VMEM((SPAN + HALO, cols), F32),
             pltpu.VMEM((SPAN, width), BF16),
         ],
+        cost_estimate=cost(10),
         name=f"unprep_{block}",
     )(*ins)
     return dict(zip(names, got))
 
 
+def finish_kernel(peer_ref, x_ref, dres_ref, half_ref, far_ref, i0_ref, i1_ref, gain_ref, out_ref):
+    rows, width = x_ref.shape
+    cols = out_ref.shape[1]
+    own = pl.ds(pl.multiple_of(peer_ref[0] * cols, cols), cols)
+    x = x_ref[...].astype(F32)
+    scale = lax.rsqrt(jnp.mean(x * x, -1, keepdims=True) + NORM_EPS)
+    inner = jnp.transpose(i0_ref[...] + i1_ref[...])[:, 0:1] / width
+    d_normed = half_ref[0].astype(F32) + far_ref[...].astype(F32)
+    d_normed = d_normed * gain_ref[0:1, own]
+    x_own = x_ref[:, own].astype(F32)
+    out_ref[...] = dres_ref[...] + scale * d_normed - x_own * (scale * scale * scale * inner)
+
+
+def finish_call(peers, x, dres, half, far, inner, inner_far, gains):
+    rows, width = x.shape
+    cols = dres.shape[1]
+    row = lambda n: pl.BlockSpec((SPAN, n), lambda i: (i, 0))
+    across = pl.BlockSpec((8, SPAN), lambda i: (0, i))
+    return pl.pallas_call(
+        finish_kernel,
+        grid=(rows // SPAN,),
+        in_specs=[
+            pl.BlockSpec(memory_space=pltpu.SMEM),
+            row(width),
+            row(cols),
+            pl.BlockSpec((1, SPAN, cols), lambda i: (0, i, 0)),
+            row(cols),
+            across,
+            across,
+            pl.BlockSpec(gains.shape, lambda i: (0, 0)),
+        ],
+        out_specs=row(cols),
+        out_shape=jax.ShapeDtypeStruct((rows, cols), F32),
+        cost_estimate=cost(4),
+        name="finish",
+    )(peers, x, dres, half, far, inner, inner_far, gains)
+
+
+def ring_of(size):
+    return [list(range(0, size, 2)) + list(range(size - 1 - size % 2, 0, -2))]
+
+
+def ring_scatter(payload, axis, size):
+    return lax.psum_scatter(
+        payload, axis, scatter_dimension=0, axis_index_groups=ring_of(size), tiled=True
+    )
+
+
+def ring_gather(part, axis, size):
+    return lax.all_gather(part, axis, axis=0, axis_index_groups=ring_of(size), tiled=True)
+
+
+def stacked_rows(pieces, full):
+    at = 0
+    for piece in pieces:
+        full = lax.dynamic_update_slice(full, piece, (at, 0))
+        at += piece.shape[0]
+    return full
+
+
+def after(value, *others):
+    return lax.optimization_barrier((value, *others))[0]
+
+
 def per_device(
+    ring_size,
     layer_input,
     proj_weight,
     conv_weight,
@@ -905,134 +1060,142 @@
     sa = sbt = None
     states, mixes = [], []
     for c in range(nb):
+        if c > 1:
+            a = after(a, *mixes[c - 2]["pieces"][1:3])
         state = dict(a=a, bt=bt, sa=sa, sbt=sbt, lg=lg)
         got = mix_call(c, nb, shift, seq_len, lg, q, k, v, kt, pers_low, gp, a, bt, sa, sbt)
         if c < nb - 1:
             a, bt, sa, sbt, state["ga"], state["gbt"] = got[4:]
         states.append(state)
-        mixes.append(dict(mixed=got[0], tot=got[1], att=got[2], linv=got[3]))
-    for mix in mixes:
-        near, far = swap(mix["mixed"], 1), swap(mix["mixed"], 2)
-        mix["all"] = (mix["mixed"], near, far, swap(far, 1))
-    names = ["res", "nt", "hid", "dgu", "pkeep", "psend", "dkeep", "dsend", "gg"]
-    ffns = []
-    for c in range(nb):
-        got = ffn_call(
-            c, peers, layer_input, mixes[c]["all"], ow, norm_gains, ffn_in, ffn_out, cot
+        far = swap(got[0], 2)
+        other = swap(got[0], 3) if c == nb - 1 else swap(far, 1)
+        pieces = (got[0], swap(got[0], 1), far, other)
+        mixes.append(dict(pieces=pieces, tot=got[1], att=got[2], linv=got[3]))
+    shared = None
+    ffns = [None] * nb
+    wait = [mixes[-1]["pieces"][0]]
+    if nb > 1:
+        wait += mixes[-2]["pieces"][1:3]
+    order = [0] + list(range(nb - 1, 0, -1))
+    for n, c in enumerate(order):
+        if n > 1:
+            wait = [ffns[order[n - 2]]["s1"]]
+        x = after(layer_input, *wait) if wait else layer_input
+        wait = []
+        shared, (res, keep, send, *room) = ffn_call(
+            c, peers, x, mixes[c]["pieces"], ow, norm_gains, ffn_in, ffn_out, cot, shared
         )
-        ffn = dict(zip(names, got))
-        s1 = (ffn["dkeep"].astype(F32) + swap(ffn["dsend"], 1).astype(F32)).astype(BF16)
-        r2 = swap(s1, 2)
-        ffn["pieces"] = (s1, r2, swap(s1, 1), swap(r2, 1))
-        part = (ffn["pkeep"].astype(F32) + swap(ffn["psend"], 1).astype(F32)).astype(BF16)
-        ffn["out"] = part[0].astype(F32) + swap(part[1], 2).astype(F32)
-        ffns.append(ffn)
-    rows_of = lambda key, axis: jnp.concatenate([f[key] for f in ffns], axis)
-    normed_two, hidden, dgu = rows_of("nt", 0), rows_of("hid", 0), rows_of("dgu", 1)
-    cot_full = jnp.transpose(cot, (1, 0, 2)).reshape(rows, width)
+        ffns[c] = dict(res=res)
+        grads_room = room[0] if room else grads_room
+        if c and c < nb - 1:
+            keep = after(keep, ffns[nb - 1]["r2"])
+        ffns[c]["s1"] = (keep.astype(F32) + swap(send, 1).astype(F32)).astype(BF16)
+        ffns[c]["r2"] = swap(ffns[c]["s1"], 2)
+    gain_two, normed_two, hidden, dgu, part_keep, part_send, cot_full, mixed_full = shared
     along_rows = (((0,), (0,)), ((), ()))
-    ffn_out_grad = lax.dot_general(hidden, cot_full, along_rows, preferred_element_type=F32)
-    ffn_in_grad = [
-        lax.dot_general(normed_two, dgu[i], along_rows, preferred_element_type=F32)
-        for i in range(2)
-    ]
-    ffn_grads = lax.psum(
-        jnp.stack([ffn_in_grad[0], ffn_in_grad[1], ffn_out_grad]).astype(BF16), "dp"
-    )
-    grads = adjoint = edge = None
-    turns, unpreps, dlgs = [None] * nb, [None] * nb, [None] * nb
+    outer = lambda left, right: lax.dot_general(
+        left, right, along_rows, preferred_element_type=F32
+    ).astype(BF16)
+    lead = ffns[nb - 1]
+    part = (part_keep.astype(F32) + swap(part_send, 1).astype(F32)).astype(BF16)
+    ffn_grads = stacked_rows(
+        [
+            outer(after(normed_two, lead["s1"], ffns[0]["r2"]), dgu[0]),
+            outer(after(normed_two, lead["r2"]), dgu[1]),
+            outer(after(hidden, part), cot_full),
+        ],
+        grads_room,
+    )
+    tie = (ffn_grads,)
+    ffn_part = ring_scatter(ffn_grads, "dp", ring_size)
+    back = unprep = None
+    gated = [None] * nb
+
+    def turn(c, turned, ties, relay_ties):
+        s1, r2 = ffns[c]["s1"], ffns[c]["r2"]
+        pieces = (s1, r2, swap(after(s1, *relay_ties), 1), swap(after(r2, *relay_ties), 1))
+        turned, gated[c] = turn_call(
+            c, peers, pieces, after(ffns[c]["res"], *ties), cot, ow, norm_gains, gp,
+            mixes[c]["tot"], turned,
+        )
+        return turned
+
+    turned = turn(nb - 1, None, tie, (lead["r2"],))
+    ffn_wait = max(nb - 2, 0)
+    part_far = swap(part[1], 2)
+    tie = ()
     for c in reversed(range(nb)):
-        dres, rescol, dbr, dga, dgp = turn_call(
-            c, peers, ffns[c]["pieces"], ffns[c]["res"], cot, ow, norm_gains, gp, mixes[c]["tot"]
+        back = back_call(
+            c, nb, shift, seq_len, q, k, v, kt, pers_low, after(gated[c][0], *tie),
+            mixes[c]["att"], mixes[c]["linv"], states[c], back, back,
         )
-        turns[c] = dict(dres=dres, rescol=rescol, dbr=dbr)
-        back = back_call(
-            c, nb, shift, seq_len, q, k, v, kt, pers_low, dga, mixes[c]["att"], mixes[c]["linv"],
-            states[c], grads, adjoint,
+        if c == nb - 1:
+            relay_ties = (back["dq"],)
+            back["dq"] = after(back["dq"], part_far)
+        if c == ffn_wait:
+            back["dq"], ffn_part = lax.optimization_barrier((back["dq"], ffn_part))
+            ffn_grads = ring_gather(ffn_part, "dp", ring_size)
+        unprep = unprep_call(
+            c, nb, shift, seq_len, peers, back, gated[c][1], pre, proj_weight, conv_weight,
+            layer_input, norm_gains, gate, mean, pers, gain_two, unprep,
         )
-        grads = adjoint = back
-        dlgs[c] = back.get("dlg")
-        unpreps[c] = unprep_call(
-            c, nb, shift, seq_len, peers, back, dgp, pre, proj_weight, conv_weight, layer_input,
-            norm_gains, edge, gate,
-        )
-        edge = unpreps[c]["edge"]
-    layer_output = jnp.concatenate(
-        [(turns[c]["rescol"] + ffns[c]["out"]).astype(BF16) for c in range(nb)], 0
-    )
-    own_gain = lax.dynamic_slice_in_dim(norm_gains[0:1], me * cols, cols, 1)
-    d_inputs = []
-    for c in range(nb):
-        up = unpreps[c]
-        half = (up["keep"].astype(F32) + swap(up["send"], 1).astype(F32)).astype(BF16)
-        d_normed = half[0].astype(F32) + swap(half[1], 2).astype(F32)
-        inner = up["inner"]
-        inner = inner + swap(inner, 1)
-        inner = (inner + swap(inner, 2))[0][:, None]
-        x = layer_input[c * SPAN : (c + 1) * SPAN].astype(F32)
-        scale = lax.rsqrt(jnp.mean(x * x, -1, keepdims=True) + NORM_EPS)
-        x_own = lax.dynamic_slice_in_dim(x, me * cols, cols, 1)
-        d_one = scale * own_gain * d_normed - x_own * (scale * scale * scale * inner / width)
-        d_inputs.append(turns[c]["dres"] + d_one)
-    input_grad = jnp.concatenate(d_inputs, 0)
-    dproj = jnp.concatenate([u["dproj"] for u in unpreps], 1)
-    proj_grad = jnp.stack(
-        [
-            lax.dot_general(nl, dproj[i], along_rows, preferred_element_type=F32)
-            for i in range(4)
-        ]
+        tie = (unprep["edge"],)
+        if c == nb - 1:
+            for other in reversed(range(c)):
+                turned = turn(other, turned, tie, relay_ties)
+                tie = ()
+            d_res, res_cols, d_branch, d_gate_all = turned
+            tie = (d_branch,)
+    gains = unprep["gains"]
+    gains = gains + sum(swap(gains, bit) for bit in (1, 2, 3))
+    cuts = [4 * width, width, 2 * cols, 16 * width // cols, 16, pers.shape[1] * 2]
+    cuts.append(2 * width // cols)
+    payload = stacked_rows(
+        [outer(nl, unprep["dproj"][i]) for i in range(4)]
+        + [outer(mixed_full, d_branch)],
+        unprep["small"],
+    )
+    payload = lax.dynamic_update_slice(
+        payload, gains.reshape(-1, cols).astype(BF16), (sum(cuts[:-1]), 0)
+    )
+    layer_output = (res_cols + part[0].astype(F32) + part_far.astype(F32)).astype(BF16)
+    tie = (payload,)
+    payload, ffn_grads = lax.optimization_barrier((payload, ffn_grads))
+    ffn_in_grad = ffn_grads[: 2 * width].astype(F32).reshape(2, width, -1)
+    ffn_out_grad = ffn_grads[2 * width :].astype(F32)
+    payload = ring_scatter(payload, "dp", ring_size)
+    half = (
+        unprep["keep"].astype(F32) + swap(after(unprep["send"], *tie), 1).astype(F32)
     ).astype(BF16)
-    dbr = jnp.concatenate([t["dbr"] for t in turns], 0)
-    out_grads = jnp.zeros((width, cols), BF16)
-    for j in range(4):
-        piece = jnp.concatenate([m["all"][j] for m in mixes], 0)
-        part = lax.dot_general(piece, dbr, along_rows, preferred_element_type=F32)
-        out_grads = lax.dynamic_update_slice(out_grads, part.astype(BF16), (peers[j] * cols, 0))
-    conv_grad = sum(u["cg"] for u in unpreps)[: 3 * taps]
-    keys = pers[0].reshape(-1, heads, head_size)
-    d_keys = grads["dp"][0].reshape(keys.shape)
-    unit = lax.rsqrt(jnp.sum(keys * keys, -1, keepdims=True) + UNIT_EPS)
-    d_keys = unit * (
-        d_keys - keys * (unit * unit * jnp.sum(d_keys * keys, -1, keepdims=True))
-    )
-    d_pers = jnp.stack([d_keys.reshape(-1, cols), grads["dp"][1]])
-    gate_grad = jnp.zeros((3 * heads, width), F32)
-    for c in range(nb - 1):
-        gate_grad = gate_grad + dlgs[c][0, : 3 * heads, None] * mean[8 * c][None, :]
-    gains = jnp.stack(
-        [sum(u["gg"][0] for u in unpreps), sum(f["gg"][0] for f in ffns)]
-    )
-    gains = gains + swap(gains, 1)
-    gains = gains + swap(gains, 2)
-    tail = [
-        proj_grad,
-        out_grads,
-        grads["ab"].astype(BF16),
-        grads["btb"].astype(BF16),
-    ]
-    small = jnp.concatenate(
-        [g.reshape(-1, cols) for g in (gate_grad, conv_grad, d_pers, gains)], 0
-    )
-    tail = lax.psum(tail, "dp")
-    small = lax.psum(small, "dp")
-    sizes = [3 * heads * width, 3 * taps * cols, d_pers.size, 2 * width]
-    cuts = [0]
-    for size in sizes:
-        cuts.append(cuts[-1] + size // cols)
-    gate_grad, conv_grad, d_pers, gains = (small[b:e] for b, e in zip(cuts, cuts[1:]))
+    inner = unprep["inner"] + swap(unprep["inner"], 1)
+    far = swap(half[1], 2)
+    input_grad = finish_call(
+        peers, layer_input, d_res, half, far, inner, swap(inner, 2), norm_gains
+    )
+    payload, input_grad, ffn_in_grad, ffn_out_grad, layer_output = lax.optimization_barrier(
+        (payload, input_grad, ffn_in_grad, ffn_out_grad, layer_output)
+    )
+    payload = ring_gather(payload, "dp", ring_size)
+    got, at = [], 0
+    for cut in cuts:
+        got.append(payload[at : at + cut].astype(F32))
+        at += cut
+    gains = got[6].reshape(2, width)
+    d_gate = jnp.concatenate(jnp.split(got[3], width // cols, 0), 1)[: 3 * heads]
+    d_pers = got[5].reshape(2, -1, heads, head_size)
     return (
         layer_output,
         input_grad,
-        tail[0].astype(F32),
-        conv_grad.reshape(3, taps, cols),
-        jnp.transpose(d_pers.reshape(2, -1, heads, head_size), (0, 2, 1, 3)),
-        tail[2].astype(F32).reshape(memory_in.shape),
-        jnp.transpose(tail[3].astype(F32).reshape(heads, head_size, mem_hid), (0, 2, 1)),
-        jnp.transpose(gate_grad.reshape(3, heads, width), (2, 0, 1)),
-        tail[1].astype(F32),
-        ffn_grads[:2].astype(F32),
-        ffn_grads[2].astype(F32),
-        gains.reshape(2, width),
+        got[0].reshape(4, width, cols),
+        got[4][: 3 * taps].reshape(3, taps, cols),
+        jnp.transpose(d_pers, (0, 2, 1, 3)),
+        got[2][:cols].reshape(memory_in.shape),
+        jnp.transpose(got[2][cols:].reshape(heads, head_size, mem_hid), (0, 2, 1)),
+        jnp.transpose(d_gate.reshape(3, heads, width), (2, 0, 1)),
+        got[1],
+        ffn_in_grad,
+        ffn_out_grad,
+        gains,
     )
 
 
@@ -1066,6 +1229,7 @@
         P("head", None),
         P(),
     )
+    body = functools.partial(per_device, mesh.shape["dp"])
     return jax.shard_map(
-        per_device, mesh=mesh, in_specs=in_specs, out_specs=out_specs, check_vma=False
-    )
+        body, mesh=mesh, in_specs=in_specs, out_specs=out_specs, check_vma=False
+    )

time: 734 us -> 409 us (0.56)
  waiting for transfers between devices: 388 us -> 102 us
  local copies, waits for them, and re-layouts: 48.2 us -> 19.8 us
  other arithmetic: 41.7 us -> 18.9 us
  Pallas kernels: 186 us -> 198 us
    psum x2 -> x0, waiting for transfers between devices: 309 us -> none  [the longest x1 276 us: per_device(): tail = lax.psum(tail, 'dp')]
    all_gather x0 -> x2, waiting for transfers between devices: none -> 55.4 us  [ring_gather(): lax.all_gather(part, axis, axis=0, axis_index_groups=ring_of(size), tiled...]
    ppermute x41 -> x30, waiting for transfers between devices: 77.5 us -> 36.1 us  [per_device(): lax.ppermute(a, 'head', [(i, i ^ bit) for i in range(count)])]
    convert_element_type x19 -> x11, other arithmetic: 23.8 us -> 9.98 us  [the longest x3 3.03 us: per_device(): got.append(payload[at:at + cut].astype(F32))]
    mul x17 -> x0, local copies, waits for them, and re-layouts: 12.8 us -> none  [the longest x12 8.55 us: per_device(): gate_grad = gate_grad + dlgs[c][0, :3 * heads, None] * mean[8 * c][None, :]]
    all_gather x1, waiting for transfers between devices: 0.01 us -> 8.7 us  [per_device(): cot = lax.all_gather(out_grad, 'head', axis=0, tiled=False)]
    unnamed x185 -> x90, local copies, waits for them, and re-layouts: 17.7 us -> 9.27 us
    pallas_call x6 -> x7, Pallas kernels: 60.6 us -> 68.9 us  [the longest x3 47.8 us: ffn_call(): pl.pallas_call(functools.partial(ffn_kernel, shared is None), grid=(steps...]
  transfers between devices with their start and end apart: 45 -> 36, of which waited for: 18 -> 13; matrix products, arithmetic and copies ran while one was open for 10% -> 10% of each run, Pallas kernels for 21% -> 45%
where the time goes in v2:
time: 409 us; the launch traced here: 401 us
  Pallas kernels  198 us (48%)
  waiting for transfers between devices  102 us (25%)
  matrix products  28.1 us (7%)
  local copies, waits for them, and re-layouts  19.8 us (5%)
  other arithmetic  18.9 us (5%)
  starting transfers between devices  18.1 us (4%)
  between operations  15.5 us (4%)
    all_gather x2, waiting for transfers between devices, ring_gather(): lax.all_gather(part, axis, axis=0, axis_index_groups=ring_of(size), tiled...  55.4 us
    pallas_call x3, Pallas kernels, back_call(): pl.pallas_call(functools.partial(back_kernel, block, nb, shift), grid=(1,...  52.9 us
    pallas_call x3, Pallas kernels, ffn_call(): pl.pallas_call(functools.partial(ffn_kernel, shared is None), grid=(steps...  47.8 us
    ppermute x30, waiting for transfers between devices, per_device(): lax.ppermute(a, 'head', [(i, i ^ bit) for i in range(count)])  36.1 us
    pallas_call x3, Pallas kernels, unprep_call(): pl.pallas_call(functools.partial(unprep_kernel, block, nb, shift), grid=(...  32.6 us
    dot_general x8, matrix products, per_device(): lax.dot_general(left, right, along_rows, preferred_element_type=F32)  28.1 us
    pallas_call x3, Pallas kernels, mix_call(): pl.pallas_call(functools.partial(mix_kernel, block, nb, shift, first, las...  27.9 us
    ppermute x30, starting transfers between devices, per_device(): lax.ppermute(a, 'head', [(i, i ^ bit) for i in range(count)])  17.8 us
  transfers between devices with their start and end apart: 36, of which 13 were waited for; matrix products, arithmetic and copies ran while one was open for 10% of the time, Pallas kernels for 45%

profile of v2, /device:TPU:0, one launch (start us, length us, event | category | flops | bytes accessed | tf_op | source)
XLA Modules:
  0.0 400.8 jit_solution(9663063002794983937)
XLA Ops:
  12.6 15.7 %prep.1 = (bf16[1536,256]{1,0:T(8,128)(2,1)}, bf16[1536,256]{1,0:T(8,128)(2,1)}, bf16[1536,256]{1,0:T(8,128)(2,1)}, bf16[256,1536]{1,0:T(8,128)(2,1)}, f32[3,153...) custom-call(s32[1]{0:T(128)S(6)} %copy.114.seq_ref.refs_0_, ...), custom_call_target="tpu_custom_call" | custom-call | flops 2249999872 | bytes 1048576 | tf_op jit(solution)/shard_map/prep/pallas_call | solution.py:146
  28.3 8.7 %mix_0.1 = (bf16[512,256]{1,0:T(8,128)(2,1)}, f32[512,256]{1,0:T(8,128)}, f32[512,256]{1,0:T(8,128)}, f32[512,256]{1,0:T(8,128)}, f32[256,256]{1,0:T(8,128)}, /*...) custom-call(s32[1]{0:T(128)S(6)} %copy.114.seq_ref.refs_0_, ...), custom_call_target="tpu_custom_call" | custom-call | flops 1350000000 | bytes 1048576 | tf_op jit(solution)/shard_map/mix_0/pallas_call | solution.py:307
  40.1 10.3 %mix_1.1 = (bf16[512,256]{1,0:T(8,128)(2,1)}, f32[512,256]{1,0:T(8,128)}, f32[512,256]{1,0:T(8,128)}, f32[512,256]{1,0:T(8,128)}, f32[256,256]{1,0:T(8,128)}, /*...) custom-call(s32[1]{0:T(128)S(6)} %copy.114.seq_ref.refs_0_, ...), custom_call_target="tpu_custom_call" | custom-call | flops 1350000000 | bytes 1048576 | tf_op jit(solution)/shard_map/mix_1/pallas_call | solution.py:307
  51.1 8.9 %mix_2.1 = (bf16[512,256]{1,0:T(8,128)(2,1)}, f32[512,256]{1,0:T(8,128)}, f32[512,256]{1,0:T(8,128)}, f32[512,256]{1,0:T(8,128)}) custom-call(s32[1]{0:T(128)S(6)} %copy.114.seq_ref.refs_0_, f32[24,128]{1,0:T(8,128)} %get-tuple-element.172.refs_1_.refs_14_, bf16[1536,256]{1,0:T(8,128)(2,1)} %get-tuple-element.167.refs_2_.refs_1_, ...), custom_call_target="tpu_custom_call" | custom-call | flops 1350000000 | bytes 1048576 | tf_op jit(solution)/shard_map/mix_2/pallas_call | solution.py:307
  65.9 8.7 %all-gather.13.cloned.1.call-done = bf16[6144,256]{1,0:T(8,128)(2,1)} async-done(((bf16[1536,256]{1,0:T(8,128)(2,1)}), bf16[6144,256]{1,0:T(8,128)(2,1)}) %all-gather.13.cloned.1.call-update) | async-done | bytes 3145744 | tf_op jit(solution)/shard_map/all_gather | solution.py:1051
  74.6 15.8 %ffn_0.1 = (f32[8,1024]{1,0:T(8,128)}, bf16[1536,1024]{1,0:T(8,128)(2,1)}, bf16[1536,1024]{1,0:T(8,128)(2,1)}, bf16[2,1536,1024]{2,1,0:T(8,128)(2,1)}, bf16[2,15...) custom-call(s32[4]{0:T(128)} %pad_add_fusion.refs_0_.refs_1_.peer_re, ...), custom_call_target="tpu_custom_call" | custom-call | flops 2249999872 | bytes 1048576 | tf_op jit(solution)/shard_map/ffn_0/pallas_call | solution.py:413
  91.4 15.8 %ffn_2.1 = (f32[8,1024]{1,0:T(8,128)}, bf16[1536,1024]{1,0:T(8,128)(2,1)}, bf16[1536,1024]{1,0:T(8,128)(2,1)}, bf16[2,1536,1024]{2,1,0:T(8,128)(2,1)}, bf16[2,15...) custom-call(s32[4]{0:T(128)} %pad_add_fusion.refs_0_.refs_1_.peer_re, ...), custom_call_target="tpu_custom_call", output_to_operand_aliasing={{0}: (11, {}), {1}: (12, {}), {2}: (13, {}), {3}: (14, {}),... | custom-call | flops 2249999872 | bytes 1048576 | tf_op jit(solution)/shard_map/ffn_2/pallas_call | solution.py:413
  116.1 16.1 %ffn_1.1 = (f32[8,1024]{1,0:T(8,128)}, bf16[1536,1024]{1,0:T(8,128)(2,1)}, bf16[1536,1024]{1,0:T(8,128)(2,1)}, bf16[2,1536,1024]{2,1,0:T(8,128)(2,1)}, bf16[2,15...) custom-call(s32[4]{0:T(128)} %pad_add_fusion.refs_0_.refs_1_.peer_re, ...), custom_call_target="tpu_custom_call", output_to_operand_aliasing={{0}: (11, {}), {1}: (12, {}), {2}: (13, {}), {3}: (14, {}),... | custom-call | flops 2249999872 | bytes 1048576 | tf_op jit(solution)/shard_map/ffn_1/pallas_call | solution.py:413
  137.1 7.9 %convert_dynamic-update-slice_fusion.2 = bf16[3072,1024]{1,0:T(8,128)(2,1)} fusion(bf16[3072,1024]{1,0:T(8,128)(2,1)} %get-tuple-element.200, bf16[1536,1024]{1,0:T(8,128)(2,1)} %get-tuple-element.213, bf16[2,1536,1024]{2,1,0:T(8,128)(2,1)} %get-tuple-element.212), kind=kOutput, calls=%fused_computation.11 | convolution fusion | flops 3222274048 | bytes 8388608 | tf_op jit(solution)/shard_map/dot_general | solution.py:1096
  145.0 4.8 %convert_dynamic-update-slice_fusion.1 = bf16[3072,1024]{1,0:T(8,128)(2,1)} fusion(bf16[3072,1024]{1,0:T(8,128)(2,1)} %convert_dynamic-update-slice_fusion.2, bf16[1536,1024]{1,0:T(8,128)(2,1)S(1)} %copy-done.4, bf16[2,1536,1024]{2,1,0:T(8,128)(2,1)S(1)} %copy-done), kind=kOutput, calls=%fused_computation.10 | convolution fusion | flops 3222274048 | bytes 8388608 | tf_op jit(solution)/shard_map/dot_general | solution.py:1096
  152.2 4.7 %convert_dynamic-update-slice_fusion = bf16[3072,1024]{1,0:T(8,128)(2,1)} fusion(bf16[3072,1024]{1,0:T(8,128)(2,1)} %convert_dynamic-update-slice_fusion.1, bf16[1536,1024]{1,0:T(8,128)(2,1)S(1)} %copy-done.5, bf16[1536,1024]{1,0:T(8,128)(2,1)S(1)} %copy-done.6), kind=kOutput, calls=%fused_computation.9 | convolution fusion | flops 3222274048 | bytes 8388608 | tf_op jit(solution)/shard_map/dot_general | solution.py:1096
  165.7 5.2 %turn_2.1 = (f32[1536,256]{1,0:T(8,128)}, f32[1536,256]{1,0:T(8,128)}, bf16[1536,256]{1,0:T(8,128)(2,1)}, bf16[1536,256]{1,0:T(8,128)(2,1)}, bf16[512,256]{1,0:T(8,128)(2,1)}, /*index=5*/bf16[512,256]{1,0:T(8,128)(2,1)}) custom-call(s32[4]{0:T(128)} %pad_add_fusion.refs_0_.refs_1_.peer_ref, bf16[512,512]{1,0:T(8,128)(2,1)} %copy-done.16, ...), custom_call_target="tpu_custom_call" | custom-call | flops 750000000 | bytes 1048576 | tf_op jit(solution)/shard_map/turn_2/pallas_call | solution.py:522
  171.0 16.7 %back_2.1 = (f32[512,256]{1,0:T(8,128)}, f32[1536,256]{1,0:T(8,128)}, f32[1536,256]{1,0:T(8,128)}, f32[2,16,256]{2,1,0:T(8,128)}, f32[256,256]{1,0:T(8,128)}, /*index=5*/f32[256,256]{1,0:T(8,128)}) custom-call(s32[1]{0:T(128)S(6)} %copy.114.seq_ref.refs_0_, bf16[1536,256]{1,0:T(8,128)(2,1)} %get-tuple-element.167.refs_2_.refs_1_, ...), custom_call_target="tpu_custom_call" | custom-call | flops 2550000128 | bytes 1048576 | tf_op jit(solution)/shard_map/back_2/pallas_call | solution.py:756
  192.0 10.0 %unprep_2.1 = (f32[16,256]{1,0:T(8,128)}, f32[8,1024]{1,0:T(8,128)}, f32[16,1024]{1,0:T(8,128)}, bf16[4,1536,256]{2,1,0:T(8,128)(2,1)}, bf16[2,1536,256]{2,1,0:T...) custom-call(s32[1]{0:T(128)S(6)} %copy.114.seq_ref.refs_0_, ...), custom_call_target="tpu_custom_call" | custom-call | flops 1500000000 | bytes 1048576 | tf_op jit(solution)/shard_map/unprep_2/pallas_call | solution.py:940
  202.0 5.1 %turn_1.1 = (f32[1536,256]{1,0:T(8,128)}, f32[1536,256]{1,0:T(8,128)}, bf16[1536,256]{1,0:T(8,128)(2,1)}, bf16[1536,256]{1,0:T(8,128)(2,1)}, bf16[512,256]{1,0:T(8,128)(2,1)}, /*index=5*/bf16[512,256]{1,0:T(8,128)(2,1)}) custom-call(s32[4]{0:T(128)} %pad_add_fusion.refs_0_.refs_1_.peer_re, ...), custom_call_target="tpu_custom_call", output_to_operand_aliasing={{0}: (11, {}), {1}: (12, {}), {2}: (13, {}), {3}: (14, {})} | custom-call | flops 750000000 | bytes 1048576 | tf_op jit(solution)/shard_map/turn_1/pallas_call | solution.py:522
  208.0 5.5 %turn_0.1 = (f32[1536,256]{1,0:T(8,128)}, f32[1536,256]{1,0:T(8,128)}, bf16[1536,256]{1,0:T(8,128)(2,1)}, bf16[1536,256]{1,0:T(8,128)(2,1)}, bf16[512,256]{1,0:T(8,128)(2,1)}, /*index=5*/bf16[512,256]{1,0:T(8,128)(2,1)}) custom-call(s32[4]{0:T(128)} %pad_add_fusion.refs_0_.refs_1_.peer_re, ...), custom_call_target="tpu_custom_call", output_to_operand_aliasing={{0}: (11, {}), {1}: (12, {}), {2}: (13, {}), {3}: (14, {})} | custom-call | flops 750000000 | bytes 1048576 | tf_op jit(solution)/shard_map/turn_0/pallas_call | solution.py:522
  213.5 19.5 %back_1.1 = (f32[512,256]{1,0:T(8,128)}, f32[1024,256]{1,0:T(8,128)}, f32[1024,256]{1,0:T(8,128)}, f32[2,16,256]{2,1,0:T(8,128)}, f32[256,256]{1,0:T(8,128)}, /*...) custom-call(s32[1]{0:T(128)S(6)} %copy.114.seq_ref.refs_0_, ...), custom_call_target="tpu_custom_call" | custom-call | flops 2550000128 | bytes 1048576 | tf_op jit(solution)/shard_map/back_1/pallas_call | solution.py:756
  233.1 10.9 %unprep_1.1 = (f32[16,256]{1,0:T(8,128)}, f32[8,1024]{1,0:T(8,128)}, f32[16,1024]{1,0:T(8,128)}, bf16[4,1536,256]{2,1,0:T(8,128)(2,1)}, bf16[2,1536,256]{2,1,0:T...) custom-call(s32[1]{0:T(128)S(6)} %copy.114.seq_ref.refs_0_, ...), custom_call_target="tpu_custom_call", output_to_operand_aliasing={{0}: (16, {}), {1}: (17, {}), {2}: (18, {}), {3}: (19, {}),... | custom-call | flops 1500000000 | bytes 1048576 | tf_op jit(solution)/shard_map/unprep_1/pallas_call | solution.py:940
  244.0 16.6 %back_0.1 = (f32[512,256]{1,0:T(8,128)}, f32[512,256]{1,0:T(8,128)}, f32[512,256]{1,0:T(8,128)}, f32[2,16,256]{2,1,0:T(8,128)}, f32[256,256]{1,0:T(8,128)}, /*index=5*/f32[256,256]{1,0:T(8,128)}, f32[8,128]{1,0:T(8,128)}) custom-call(s32[1]{0:T(128)S(6)} %copy.114.seq_ref.refs_0_, bf16[1536,256]{1,0:T(8,128)(2,1)} %get-tuple-element.167.refs_2_.refs_1_, ...), custom_call_target="tpu_custom_call" | custom-call | flops 2550000128 | bytes 1048576 | tf_op jit(solution)/shard_map/back_0/pallas_call | solution.py:756
  260.7 11.6 %unprep_0.1 = (f32[16,256]{1,0:T(8,128)}, f32[8,1024]{1,0:T(8,128)}, f32[16,1024]{1,0:T(8,128)}, bf16[4,1536,256]{2,1,0:T(8,128)(2,1)}, bf16[2,1536,256]{2,1,0:T...) custom-call(s32[1]{0:T(128)S(6)} %copy.114.seq_ref.refs_0_, ...), custom_call_target="tpu_custom_call", output_to_operand_aliasing={{0}: (20, {}), {1}: (21, {}), {2}: (22, {}), {3}: (23, {}),... | custom-call | flops 1500000000 | bytes 1048576 | tf_op jit(solution)/shard_map/unprep_0/pallas_call | solution.py:940
  286.2 15.9 %all-gather.7.cloned.1.call-done = bf16[3072,1024]{1,0:T(8,128)(2,1)} async-done(((bf16[384,1024]{1,0:T(8,128)(2,1)}), bf16[3072,1024]{1,0:T(8,128)(2,1)}) %all-gather.7.cloned.1.call-update) | async-done | bytes 6291472 | tf_op jit(solution)/shard_map/all_gather | solution.py:1007
  310.8 16.1 %collective-permute-done.29.i1_ref = f32[8,1536]{1,0:T(8,128)S(1)} collective-permute-done((f32[8,1536]{1,0:T(8,128)S(1)}, f32[8,1536]{1,0:T(8,128)S(1)}, u32[]{:S(2)}, u32[]{:S(2)}) %collective-permute-start.29) | collective-permute-done | bytes 49184 | tf_op jit(solution)/shard_map/ppermute | solution.py:1049
  327.8 5.3 %finish.1 = f32[1536,256]{1,0:T(8,128)} custom-call(s32[4]{0:T(128)} %pad_add_fusion.refs_0_.refs_1_.peer_ref, bf16[1536,1024]{1,0:T(8,128)(2,1)} %x_ref.3, f32[1536,256]{1,0:T(8,128)} %get-tuple-element.310.dres_ref, bf16[2,1536,256]{2,1,0:T(8,128)(2,1)} %copy-done.9, bf16[1536,256]{1,0:T(8,128)(2,1)} %copy-done.18, f32[8,1536]{1,0:T(8,128)} %copy-done.37, ...), custom_call_target="tpu_custom_call" | custom-call | flops 600000000 | bytes 1048576 | tf_op jit(solution)/shard_map/finish/pallas_call | solution.py:976
  343.1 39.5 %all-gather.9.cloned.1.call-done = bf16[6144,256]{1,0:T(8,128)(2,1)} async-done(((bf16[768,256]{1,0:T(8,128)(2,1)}), bf16[6144,256]{1,0:T(8,128)(2,1)}) %all-gather.9.cloned.1.call-update) | async-done | bytes 3145744 | tf_op jit(solution)/shard_map/all_gather | solution.py:1007
  (208 shorter events, 89.8 us)
Async XLA Ops:
  7.2 58.7 %all-gather.11.cloned.1.call-start = ((), (), s32[]{:S(2)}) async-start(), calls=%async_computation.6 | async-start | bytes 2621440 | tf_op jit(solution)/shard_map/all_gather | solution.py:1050
  7.9 66.7 %all-gather.13.cloned.1.call-start = ((), (), s32[]{:S(2)}) async-start(), calls=%async_computation.7 | async-start | bytes 3932160 | tf_op jit(solution)/shard_map/all_gather | solution.py:1051
  8.7 224.4 %reduce-scatter.3.cloned.1.call-start = ((), (), s32[]{:S(2)}) async-start(), calls=%async_computation.2 | async-start | bytes 7077888 | tf_op jit(solution)/shard_map/reduce_scatter | solution.py:1001
  37.0 14.0 %collective-permute-start.1 = (bf16[512,256]{1,0:T(8,128)(2,1)}, bf16[512,256]{1,0:T(8,128)(2,1)S(1)}, u32[]{:S(2)}, u32[]{:S(2)}) collective-permute-start(bf16[512,256]{1,0:T(8,128)(2,1)} %get-tuple-element.179.refs_2_), channel_id=1, source_target_pairs={{0,2},{1,3},{2,0},{3,1},{4,6},{5,7},{6,4},{7,5},{8,10},{9,11},{10,... | collective-permute-start | bytes 786440 | tf_op jit(solution)/shard_map/ppermute | solution.py:1049
  50.9 15.0 %collective-permute-start.3 = (bf16[512,256]{1,0:T(8,128)(2,1)}, bf16[512,256]{1,0:T(8,128)(2,1)S(1)}, u32[]{:S(2)}, u32[]{:S(2)}) collective-permute-start(bf16[512,256]{1,0:T(8,128)(2,1)} %get-tuple-element.183.refs_2_), channel_id=1, source_target_pairs={{0,2},{1,3},{2,0},{3,1},{4,6},{5,7},{6,4},{7,5},{8,10},{9,11},{10,... | collective-permute-start | bytes 786440 | tf_op jit(solution)/shard_map/ppermute | solution.py:1049
  51.0 14.9 %collective-permute-start.4 = (bf16[512,256]{1,0:T(8,128)(2,1)S(1)}, bf16[512,256]{1,0:T(8,128)(2,1)S(1)}, u32[]{:S(2)}, u32[]{:S(2)}) collective-permute-start(bf16[512,256]{1,0:T(8,128)(2,1)S(1)} %collective-permute-done.1.refs_4_), channel_id=1, source_target_pairs={{0,1},{1,0},{2,3},{3,2},{4,5},{5,4},{6,7},{7,6},{8,9},{9,8},{10,11... | collective-permute-start | bytes 786440 | tf_op jit(solution)/shard_map/ppermute | solution.py:1049
  60.0 30.5 %collective-permute-start.7 = (bf16[512,256]{1,0:T(8,128)(2,1)}, bf16[512,256]{1,0:T(8,128)(2,1)S(1)}, u32[]{:S(2)}, u32[]{:S(2)}) collective-permute-start(bf16[512,256]{1,0:T(8,128)(2,1)} %get-tuple-element.182.refs_2_), channel_id=1, source_target_pairs={{0,1},{1,0},{2,3},{3,2},{4,5},{5,4},{6,7},{7,6},{8,9},{9,8},{10,11... | collective-permute-start | bytes 786440 | tf_op jit(solution)/shard_map/ppermute | solution.py:1049
  60.4 30.1 %collective-permute-start.8 = (bf16[512,256]{1,0:T(8,128)(2,1)}, bf16[512,256]{1,0:T(8,128)(2,1)S(1)}, u32[]{:S(2)}, u32[]{:S(2)}) collective-permute-start(bf16[512,256]{1,0:T(8,128)(2,1)} %get-tuple-element.182.refs_2_), channel_id=1, source_target_pairs={{0,2},{1,3},{2,0},{3,1},{4,6},{5,7},{6,4},{7,5},{8,10},{9,11},{10,... | collective-permute-start | bytes 786440 | tf_op jit(solution)/shard_map/ppermute | solution.py:1049
  62.3 28.2 %collective-permute-start.9 = (bf16[512,256]{1,0:T(8,128)(2,1)}, bf16[512,256]{1,0:T(8,128)(2,1)S(1)}, u32[]{:S(2)}, u32[]{:S(2)}) collective-permute-start(bf16[512,256]{1,0:T(8,128)(2,1)} %get-tuple-element.182.refs_2_), channel_id=1, source_target_pairs={{0,3},{1,2},{2,1},{3,0},{4,7},{5,6},{6,5},{7,4},{8,11},{9,10},{10,... | collective-permute-start | bytes 786440 | tf_op jit(solution)/shard_map/ppermute | solution.py:1049
  110.5 21.9 %collective-permute-start.11 = (bf16[512,512]{1,0:T(8,128)(2,1)S(1)}, bf16[512,512]{1,0:T(8,128)(2,1)}, u32[]{:S(2)}, u32[]{:S(2)}) collective-permute-start(bf16[512,512]{1,0:T(8,128)(2,1)S(1)} %add_convert_fusion.3.refs_1_), channel_id=1, source_target_pairs={{0,2},{1,3},{2,0},{3,1},{4,6},{5,7},{6,4},{7,5},{8,10},{9,11},{10,... | collective-permute-start | bytes 1572872 | tf_op jit(solution)/shard_map/ppermute | solution.py:1049
  113.7 23.4 %collective-permute-start.6 = (bf16[512,512]{1,0:T(8,128)(2,1)S(1)}, bf16[512,512]{1,0:T(8,128)(2,1)S(1)}, u32[]{:S(2)}, u32[]{:S(2)}) collective-permute-start(bf16[512,512]{1,0:T(8,128)(2,1)S(1)} %add_convert_fusion.4.refs_1_), channel_id=1, source_target_pairs={{0,2},{1,3},{2,0},{3,1},{4,6},{5,7},{6,4},{7,5},{8,10},{9,11},{10,... | collective-permute-start | bytes 1572872 | tf_op jit(solution)/shard_map/ppermute | solution.py:1049
  132.2 17.6 %collective-permute-start.15 = (bf16[2,1536,256]{2,1,0:T(8,128)(2,1)}, bf16[2,1536,256]{2,1,0:T(8,128)(2,1)S(1)}, u32[]{:S(2)}, u32[]{:S(2)}) collective-permute-start(bf16[2,1536,256]{2,1,0:T(8,128)(2,1)} %get-tuple-element.216), channel_id=1, source_target_pairs={{0,1},{1,0},{2,3},{3,2},{4,5},{5,4},{6,7},{7,6},{8,9},{9,8},{10,11... | collective-permute-start | bytes 4718600 | tf_op jit(solution)/shard_map/ppermute | solution.py:1049
  157.0 145.1 %all-gather.7.cloned.1.call-start = ((), (), s32[]{:S(2)}) async-start(), calls=%async_computation.3 | async-start | bytes 7077888 | tf_op jit(solution)/shard_map/all_gather | solution.py:1007
  161.1 26.6 %collective-permute-start.19 = (bf16[512,512]{1,0:T(8,128)(2,1)S(1)}, bf16[512,512]{1,0:T(8,128)(2,1)}, u32[]{:S(2)}, u32[]{:S(2)}) collective-permute-start(bf16[512,512]{1,0:T(8,128)(2,1)S(1)} %add_convert_fusion.2.refs_1_), channel_id=1, source_target_pairs={{0,2},{1,3},{2,0},{3,1},{4,6},{5,7},{6,4},{7,5},{8,10},{9,11},{10,... | collective-permute-start | bytes 1572872 | tf_op jit(solution)/shard_map/ppermute | solution.py:1049
  163.8 28.1 %collective-permute-start.22 = (bf16[1536,256]{1,0:T(8,128)(2,1)}, bf16[1536,256]{1,0:T(8,128)(2,1)S(1)}, u32[]{:S(2)}, u32[]{:S(2)}) collective-permute-start(bf16[1536,256]{1,0:T(8,128)(2,1)} %slice_bitcast_fusion.2), channel_id=1, source_target_pairs={{0,2},{1,3},{2,0},{3,1},{4,6},{5,7},{6,4},{7,5},{8,10},{9,11},{10,... | collective-permute-start | bytes 2359304 | tf_op jit(solution)/shard_map/ppermute | solution.py:1049
  187.7 14.3 %collective-permute-start.21 = (bf16[512,512]{1,0:T(8,128)(2,1)}, bf16[512,512]{1,0:T(8,128)(2,1)}, u32[]{:S(2)}, u32[]{:S(2)}) collective-permute-start(bf16[512,512]{1,0:T(8,128)(2,1)} %collective-permute-done.19.refs_2_), channel_id=1, source_target_pairs={{0,1},{1,0},{2,3},{3,2},{4,5},{5,4},{6,7},{7,6},{8,9},{9,8},{10,11... | collective-permute-start | bytes 1572872 | tf_op jit(solution)/shard_map/ppermute | solution.py:1049
  187.8 14.2 %collective-permute-start.20 = (bf16[512,512]{1,0:T(8,128)(2,1)S(1)}, bf16[512,512]{1,0:T(8,128)(2,1)}, u32[]{:S(2)}, u32[]{:S(2)}) collective-permute-start(bf16[512,512]{1,0:T(8,128)(2,1)S(1)} %add_convert_fusion.2.refs_1_), channel_id=1, source_target_pairs={{0,1},{1,0},{2,3},{3,2},{4,5},{5,4},{6,7},{7,6},{8,9},{9,8},{10,11... | collective-permute-start | bytes 1572872 | tf_op jit(solution)/shard_map/ppermute | solution.py:1049
  188.3 18.9 %collective-permute-start.17 = (bf16[512,512]{1,0:T(8,128)(2,1)S(1)}, bf16[512,512]{1,0:T(8,128)(2,1)S(1)}, u32[]{:S(2)}, u32[]{:S(2)}) collective-permute-start(bf16[512,512]{1,0:T(8,128)(2,1)S(1)} %copy-done.22), channel_id=1, source_target_pairs={{0,1},{1,0},{2,3},{3,2},{4,5},{5,4},{6,7},{7,6},{8,9},{9,8},{10,11... | collective-permute-start | bytes 1572872 | tf_op jit(solution)/shard_map/ppermute | solution.py:1049
  188.4 18.8 %collective-permute-start.16 = (bf16[512,512]{1,0:T(8,128)(2,1)S(1)}, bf16[512,512]{1,0:T(8,128)(2,1)}, u32[]{:S(2)}, u32[]{:S(2)}) collective-permute-start(bf16[512,512]{1,0:T(8,128)(2,1)S(1)} %add_convert_fusion.4.refs_1_), channel_id=1, source_target_pairs={{0,1},{1,0},{2,3},{3,2},{4,5},{5,4},{6,7},{7,6},{8,9},{9,8},{10,11... | collective-permute-start | bytes 1572872 | tf_op jit(solution)/shard_map/ppermute | solution.py:1049
  233.1 110.0 %reduce-scatter.5.cloned.1.call-start = ((), (), s32[]{:S(2)}) async-start(), calls=%async_computation.4 | async-start | bytes 3538944 | tf_op jit(solution)/shard_map/reduce_scatter | solution.py:1001
  272.3 13.2 %collective-permute-start.23 = (f32[2,1024]{1,0:T(2,128)}, f32[2,1024]{1,0:T(2,128)S(1)}, u32[]{:S(2)}, u32[]{:S(2)}) collective-permute-start(f32[2,1024]{1,0:T(2,128)} %get-tuple-element.307), channel_id=1, source_target_pairs={{0,1},{1,0},{2,3},{3,2},{4,5},{5,4},{6,7},{7,6},{8,9},{9,8},{10,11... | collective-permute-start | bytes 24584 | tf_op jit(solution)/shard_map/ppermute | solution.py:1049
  302.1 80.5 %all-gather.9.cloned.1.call-start = ((), (), s32[]{:S(2)}) async-start(), calls=%async_computation.5 | async-start | bytes 3538944 | tf_op jit(solution)/shard_map/all_gather | solution.py:1007
  306.2 20.7 %collective-permute-start.27 = (bf16[1536,256]{1,0:T(8,128)(2,1)S(1)}, bf16[1536,256]{1,0:T(8,128)(2,1)S(1)}, u32[]{:S(2)}, u32[]{:S(2)}) collective-permute-start(bf16[1536,256]{1,0:T(8,128)(2,1)S(1)} %slice_bitcast_fusion.1), channel_id=1, source_target_pairs={{0,2},{1,3},{2,0},{3,1},{4,6},{5,7},{6,4},{7,5},{8,10},{9,11},{10,... | collective-permute-start | bytes 2359304 | tf_op jit(solution)/shard_map/ppermute | solution.py:1049
  309.0 17.9 %collective-permute-start.29 = (f32[8,1536]{1,0:T(8,128)S(1)}, f32[8,1536]{1,0:T(8,128)S(1)}, u32[]{:S(2)}, u32[]{:S(2)}) collective-permute-start(f32[8,1536]{1,0:T(8,128)S(1)} %add.47.i0_ref), channel_id=1, source_target_pairs={{0,2},{1,3},{2,0},{3,1},{4,6},{5,7},{6,4},{7,5},{8,10},{9,11},{10,... | collective-permute-start | bytes 147464 | tf_op jit(solution)/shard_map/ppermute | solution.py:1049
  (59 other events, 610.4 us)
Sparse Core Ops, SparseCore 0:
  9.6 25.2 all-gather.10
  36.4 38.1 all-gather.12
  157.1 69.5 reduce-scatter.2
  233.2 68.8 all-gather.6
  304.2 38.7 reduce-scatter.4
  344.4 38.1 all-gather.8
